TPU v7x, 32 devices: a whole 2x2x4 slice. The times are simulated.
32 devices in a mesh: gx: 4 (over x, core), gy: 8 (over z, y).
Axes of the slice: x: 2, y: 2, z: 4, core: 2. Of those that a mesh axis runs over, the one named last changes fastest.
Arguments:
- tokens: bfloat16 [4096, 2048], P('gy', 'gx'), may hold values from -6 to 6
- attn_gain: bfloat16 [2048], P('gy'), may hold values from 0.099609375 to 1.8984375
- attn_shift: bfloat16 [2048], P('gy'), may hold values from -3 to 3
- ffn_gain: bfloat16 [2048], P('gy'), may hold values from 0.099609375 to 1.8984375
- ffn_shift: bfloat16 [2048], P('gy'), may hold values from -3 to 3
- qkv_weight: bfloat16 [2048, 6144], P('gy', 'gx'), may hold values from -1 to 1
- qkv_bias: bfloat16 [6144], P(('gx', 'gy')), may hold values from -3 to 3
- out_weight: bfloat16 [2048, 2048], P('gx', 'gy'), may hold values from -6 to 6
- out_bias: bfloat16 [2048], P(('gx', 'gy')), may hold values from -3 to 3
- up_weight: bfloat16 [2048, 8192], P('gy', 'gx'), may hold values from -0.125 to 0.125
- up_bias: bfloat16 [8192], P(('gx', 'gy')), may hold values from -3 to 3
- down_weight: bfloat16 [8192, 2048], P('gx', 'gy'), may hold values from -0.0625 to 0.0625
- down_bias: bfloat16 [2048], P(('gx', 'gy')), may hold values from -3 to 3
- cotangent: bfloat16 [4096, 2048], P('gy', 'gx'), may hold values from -6 to 6
Outputs:
- output: bfloat16 [4096, 2048], P('gy', 'gx')
- grad_tokens: float32 [4096, 2048], P('gy', 'gx')
- grad_attn_gain: float32 [2048], P('gy')
- grad_attn_shift: float32 [2048], P('gy')
- grad_ffn_gain: float32 [2048], P('gy')
- grad_ffn_shift: float32 [2048], P('gy')
- grad_qkv_weight: float32 [2048, 6144], P('gy', 'gx')
- grad_qkv_bias: float32 [6144], P(('gx', 'gy'))
- grad_out_weight: float32 [2048, 2048], P('gx', 'gy')
- grad_out_bias: float32 [2048], P(('gx', 'gy'))
- grad_up_weight: float32 [2048, 8192], P('gy', 'gx')
- grad_up_bias: float32 [8192], P(('gx', 'gy'))
- grad_down_weight: float32 [8192, 2048], P('gx', 'gy')
- grad_down_bias: float32 [2048], P(('gx', 'gy'))
All inputs are finite; a program needn't handle non-finite values.
Results may differ from a plain program's by a relative error of at most 0.025.
Values may be sent and summed in bfloat16 or wider, within the bound.
A program may use at most 192 MiB of HBM per device.

v0:
```python
import jax
import jax.numpy as jnp
from jax import lax
from jax.sharding import PartitionSpec as P

HEAD = 256
ROT = 64
SPAN = 8


eps_norm = 1e-05


def passed_along(value, axis, steps):
    count = lax.axis_size(axis)
    leading, last = (max(0, -steps), min(count, count - steps))
    return lax.ppermute(value, axis, [(source, source + steps) for source in range(leading, last)])


def norm_rows(values, gain, shift):
    average = jnp.mean(values, axis=-1, keepdims=True)
    centred = values - average
    spread = jnp.mean(centred * centred, axis=-1, keepdims=True)
    return centred * lax.rsqrt(spread + eps_norm) * gain + shift


def exact_gelu(values):
    return jax.nn.gelu(values, approximate=False)


def angle_table(positions):
    half_rot = ROT // 2
    frequency = 10000.0 ** (-(2.0 * jnp.arange(half_rot).astype(jnp.float32)) / ROT)
    return positions.astype(jnp.float32)[:, None] * frequency[None, :]


def rotate(heads, angles):
    half_rot = angles.shape[-1]
    cosine = jnp.cos(angles)[:, None, :]
    sine = jnp.sin(angles)[:, None, :]
    first = heads[..., :half_rot]
    second = heads[..., half_rot : 2 * half_rot]
    return jnp.concatenate(
        [
            first * cosine - second * sine,
            second * cosine + first * sine,
            heads[..., 2 * half_rot :],
        ],
        axis=-1,
    )


def unrotate(heads, angles):
    half_rot = angles.shape[-1]
    cosine = jnp.cos(angles)[:, None, :]
    sine = jnp.sin(angles)[:, None, :]
    first = heads[..., :half_rot]
    second = heads[..., half_rot : 2 * half_rot]
    return jnp.concatenate(
        [
            first * cosine + second * sine,
            second * cosine - first * sine,
            heads[..., 2 * half_rot :],
        ],
        axis=-1,
    )


def contract_last(left, right):
    return lax.dot_general(
        left, right, (((1,), (1,)), ((), ())), preferred_element_type=jnp.float32
    )


def contract_first(left, right):
    return lax.dot_general(
        left, right, (((0,), (0,)), ((), ())), preferred_element_type=jnp.float32
    )


def visible_mask(query_pos, key_pos, seq_len):
    return (
        (key_pos[None, :] <= query_pos[:, None])
        & (key_pos >= 0)[None, :]
        & (query_pos < seq_len)[:, None]
    )


def pair_grads(
    query_set, grad_set, log_total, delta, query_pos, key_set, value_set, key_pos, seq_len
):
    factor = HEAD ** (-0.5)
    scores = (
        jnp.einsum("qhd,khd->hqk", query_set, key_set, preferred_element_type=jnp.float32) * factor
    )
    visible = visible_mask(query_pos, key_pos, seq_len)
    probs = jnp.where(
        visible[None], jnp.exp(jnp.where(visible[None], scores - log_total[:, :, None], 0.0)), 0.0
    )
    grad_probs = jnp.einsum("qhd,khd->hqk", grad_set, value_set, preferred_element_type=jnp.float32)
    grad_scores = (probs * (grad_probs - delta[:, :, None])).astype(jnp.bfloat16)
    grad_q = (
        jnp.einsum("hqk,khd->qhd", grad_scores, key_set, preferred_element_type=jnp.float32)
        * factor
    )
    grad_k = (
        jnp.einsum("hqk,qhd->khd", grad_scores, query_set, preferred_element_type=jnp.float32)
        * factor
    )
    grad_v = jnp.einsum(
        "hqk,qhd->khd", probs.astype(jnp.bfloat16), grad_set, preferred_element_type=jnp.float32
    )
    return (grad_q, grad_k, grad_v)


def local(
    tokens,
    attn_gain,
    attn_shift,
    ffn_gain,
    ffn_shift,
    qkv_weight,
    qkv_bias,
    out_weight,
    out_bias,
    up_weight,
    up_bias,
    down_weight,
    down_bias,
    cotangent,
):
    tok_rows = tokens.shape[0]
    width_part = tokens.shape[1]
    local_heads = qkv_weight.shape[1] // (3 * HEAD)
    factor = HEAD ** (-0.5)
    seq_len = tok_rows * SPAN
    local_start = lax.axis_index("gy") % SPAN * tok_rows
    positions = local_start + jnp.arange(tok_rows, dtype=jnp.int32)
    angles = angle_table(positions)
    full_rows = lax.all_gather(tokens, "gx", axis=1, tiled=True).astype(jnp.float32)
    qkv_full, up_full, qkv_shift, up_shift, gain_attn, shift_attn, gain_ffn, shift_ffn = (
        lax.all_gather(qkv_weight, "gy", axis=0, tiled=True),
        lax.all_gather(up_weight, "gy", axis=0, tiled=True),
        lax.all_gather(qkv_bias, "gy", axis=0, tiled=True),
        lax.all_gather(up_bias, "gy", axis=0, tiled=True),
        lax.all_gather(attn_gain, "gy", axis=0, tiled=True),
        lax.all_gather(attn_shift, "gy", axis=0, tiled=True),
        lax.all_gather(ffn_gain, "gy", axis=0, tiled=True),
        lax.all_gather(ffn_shift, "gy", axis=0, tiled=True),
    )
    normed_attn, back_attn = jax.vjp(
        norm_rows, full_rows, gain_attn.astype(jnp.float32), shift_attn.astype(jnp.float32)
    )
    normed_ffn, back_ffn = jax.vjp(
        norm_rows, full_rows, gain_ffn.astype(jnp.float32), shift_ffn.astype(jnp.float32)
    )
    normed_attn = normed_attn.astype(jnp.bfloat16)
    normed_ffn = normed_ffn.astype(jnp.bfloat16)
    mixed = jnp.dot(normed_attn, qkv_full, preferred_element_type=jnp.float32) + qkv_shift.astype(
        jnp.float32
    )
    mixed = mixed.reshape(tok_rows, local_heads, 3, HEAD)
    queries = rotate(mixed[:, :, 0], angles).astype(jnp.bfloat16)
    keys = rotate(mixed[:, :, 1], angles).astype(jnp.bfloat16)
    values = mixed[:, :, 2].astype(jnp.bfloat16)
    head_cols = local_heads * HEAD

    def attend_piece(carried, piece_keys, piece_values, offset):
        row_max, row_total, summed = carried
        length = piece_keys.shape[0]
        scores = (
            jnp.einsum("qhd,khd->hqk", queries, piece_keys, preferred_element_type=jnp.float32)
            * factor
        )
        visible = visible_mask(positions, offset + jnp.arange(length, dtype=jnp.int32), seq_len)
        scores = jnp.where(visible[None], scores, -1e30)
        new_max = jnp.maximum(row_max, jnp.max(scores, axis=-1))
        weights = jnp.where(visible[None], jnp.exp(scores - new_max[:, :, None]), 0.0)
        shrink = jnp.exp(row_max - new_max)
        row_total = row_total * shrink + jnp.sum(weights, axis=-1)
        summed = summed * jnp.transpose(shrink)[:, :, None] + jnp.einsum(
            "hqk,khd->qhd",
            weights.astype(jnp.bfloat16),
            piece_values,
            preferred_element_type=jnp.float32,
        )
        return (new_max, row_total, summed)

    start_state = (
        jnp.full((local_heads, tok_rows), -1e30, jnp.float32),
        jnp.zeros((local_heads, tok_rows), jnp.float32),
        jnp.zeros((tok_rows, local_heads, HEAD), jnp.float32),
    )
    state = attend_piece(start_state, keys, values, local_start)
    kv_stack = jnp.stack(
        [keys.reshape(tok_rows, head_cols), values.reshape(tok_rows, head_cols)], axis=0
    )
    for step in range(1, SPAN):
        arrived = passed_along(kv_stack, "gy", step)
        state = attend_piece(
            state,
            arrived[0].reshape(tok_rows, local_heads, HEAD),
            arrived[1].reshape(tok_rows, local_heads, HEAD),
            local_start - step * tok_rows,
        )
    row_max, row_total, summed = state
    log_total = row_max + jnp.log(row_total)
    context_sum = summed / jnp.transpose(row_total)[:, :, None]
    context_low = context_sum.reshape(tok_rows, head_cols).astype(jnp.bfloat16)
    out_full, down_full, out_cols, down_cols = (
        lax.all_gather(out_weight, "gy", axis=1, tiled=True),
        lax.all_gather(down_weight, "gy", axis=1, tiled=True),
        lax.all_gather(out_bias, "gy", axis=0, tiled=True),
        lax.all_gather(down_bias, "gy", axis=0, tiled=True),
    )
    hidden_pre = jnp.dot(normed_ffn, up_full, preferred_element_type=jnp.float32) + up_shift.astype(
        jnp.float32
    )
    hidden, gelu_back = jax.vjp(exact_gelu, hidden_pre)
    hidden_low = hidden.astype(jnp.bfloat16)
    branch_sum = jnp.dot(context_low, out_full, preferred_element_type=jnp.float32) + jnp.dot(
        hidden_low, down_full, preferred_element_type=jnp.float32
    )
    mixed_out = lax.psum_scatter(
        branch_sum.astype(jnp.bfloat16), "gx", scatter_dimension=1, tiled=True
    ).astype(jnp.float32)
    output = (
        tokens.astype(jnp.float32)
        + mixed_out
        + out_cols.astype(jnp.float32)
        + down_cols.astype(jnp.float32)
    ).astype(jnp.bfloat16)
    grad_rows = lax.all_gather(cotangent, "gx", axis=1, tiled=True)
    grad_context = contract_last(grad_rows, out_full).astype(jnp.bfloat16)
    grad_hidden = contract_last(grad_rows, down_full)
    grad_pre = gelu_back(grad_hidden)[0].astype(jnp.bfloat16)
    grad_out_local = contract_first(context_low, grad_rows)
    grad_down_local = contract_first(hidden_low, grad_rows)
    grad_bias_cols = jnp.sum(cotangent.astype(jnp.float32), axis=0)
    grad_out_w, grad_down_w, grad_bias = (
        lax.psum_scatter(
            grad_out_local.astype(jnp.bfloat16), "gy", scatter_dimension=1, tiled=True
        ).astype(jnp.float32),
        lax.psum_scatter(
            grad_down_local.astype(jnp.bfloat16), "gy", scatter_dimension=1, tiled=True
        ).astype(jnp.float32),
        lax.psum_scatter(
            grad_bias_cols.astype(jnp.bfloat16), "gy", scatter_dimension=0, tiled=True
        ).astype(jnp.float32),
    )
    grad_heads = grad_context.reshape(tok_rows, local_heads, HEAD)
    delta = jnp.einsum("qhd,qhd->hq", grad_heads.astype(jnp.float32), context_sum)
    grad_q, grad_k, grad_v = pair_grads(
        queries, grad_heads, log_total, delta, positions, keys, values, positions, seq_len
    )
    row_stack = jnp.stack(
        [
            queries.reshape(tok_rows, head_cols),
            grad_context,
            keys.reshape(tok_rows, head_cols),
            values.reshape(tok_rows, head_cols),
        ],
        axis=0,
    )
    stat_stack = jnp.stack([log_total, delta], axis=0)
    for step in [item for item in range(1 - SPAN, SPAN) if item != 0]:
        arrived = passed_along(row_stack, "gy", step)
        stats = passed_along(stat_stack, "gy", step)
        piece_pos = local_start - step * tok_rows + jnp.arange(tok_rows, dtype=jnp.int32)
        other_q = arrived[0].reshape(tok_rows, local_heads, HEAD)
        other_g = arrived[1].reshape(tok_rows, local_heads, HEAD)
        other_k = arrived[2].reshape(tok_rows, local_heads, HEAD)
        other_v = arrived[3].reshape(tok_rows, local_heads, HEAD)
        if step > 0:
            part_q, unused_k, unused_v = pair_grads(
                queries,
                grad_heads,
                log_total,
                delta,
                positions,
                other_k,
                other_v,
                piece_pos,
                seq_len,
            )
            grad_q = grad_q + part_q
        else:
            unused_q, part_k, part_v = pair_grads(
                other_q, other_g, stats[0], stats[1], piece_pos, keys, values, positions, seq_len
            )
            grad_k = grad_k + part_k
            grad_v = grad_v + part_v
    grad_mixed = jnp.stack([unrotate(grad_q, angles), unrotate(grad_k, angles), grad_v], axis=2)
    grad_mixed = grad_mixed.reshape(tok_rows, 3 * head_cols).astype(jnp.bfloat16)
    grad_norm_attn = contract_last(grad_mixed, qkv_full)
    grad_norm_ffn = contract_last(grad_pre, up_full)
    sum_attn, sum_ffn = (
        lax.psum(grad_norm_attn.astype(jnp.bfloat16), "gx").astype(jnp.float32),
        lax.psum(grad_norm_ffn.astype(jnp.bfloat16), "gx").astype(jnp.float32),
    )
    input_attn, gain_grad_attn, shift_grad_attn = back_attn(sum_attn)
    input_ffn, gain_grad_ffn, shift_grad_ffn = back_ffn(sum_ffn)
    own_cols = lax.dynamic_slice_in_dim(
        input_attn + input_ffn, lax.axis_index("gx") * width_part, width_part, 1
    )
    grad_tokens = cotangent.astype(jnp.float32) + own_cols
    grad_qkv_local = contract_first(normed_attn, grad_mixed)
    grad_up_local = contract_first(normed_ffn, grad_pre)
    grad_qkv_cols = jnp.sum(grad_mixed.astype(jnp.float32), axis=0)
    grad_up_cols = jnp.sum(grad_pre.astype(jnp.float32), axis=0)
    (
        grad_qkv_w,
        grad_up_w,
        grad_qkv_b,
        grad_up_b,
        grad_gain_attn,
        grad_shift_attn,
        grad_gain_ffn,
        grad_shift_ffn,
    ) = (
        lax.psum_scatter(
            grad_qkv_local.astype(jnp.bfloat16), "gy", scatter_dimension=0, tiled=True
        ).astype(jnp.float32),
        lax.psum_scatter(
            grad_up_local.astype(jnp.bfloat16), "gy", scatter_dimension=0, tiled=True
        ).astype(jnp.float32),
        lax.psum_scatter(
            grad_qkv_cols.astype(jnp.bfloat16), "gy", scatter_dimension=0, tiled=True
        ).astype(jnp.float32),
        lax.psum_scatter(
            grad_up_cols.astype(jnp.bfloat16), "gy", scatter_dimension=0, tiled=True
        ).astype(jnp.float32),
        lax.psum_scatter(
            gain_grad_attn.astype(jnp.bfloat16), "gy", scatter_dimension=0, tiled=True
        ).astype(jnp.float32),
        lax.psum_scatter(
            shift_grad_attn.astype(jnp.bfloat16), "gy", scatter_dimension=0, tiled=True
        ).astype(jnp.float32),
        lax.psum_scatter(
            gain_grad_ffn.astype(jnp.bfloat16), "gy", scatter_dimension=0, tiled=True
        ).astype(jnp.float32),
        lax.psum_scatter(
            shift_grad_ffn.astype(jnp.bfloat16), "gy", scatter_dimension=0, tiled=True
        ).astype(jnp.float32),
    )
    return (
        output,
        grad_tokens,
        grad_gain_attn,
        grad_shift_attn,
        grad_gain_ffn,
        grad_shift_ffn,
        grad_qkv_w,
        grad_qkv_b,
        grad_out_w,
        grad_bias,
        grad_up_w,
        grad_up_b,
        grad_down_w,
        grad_bias,
    )


def solution(mesh):
    placed = (
        P("gy", "gx"),
        P("gy"),
        P("gy"),
        P("gy"),
        P("gy"),
        P("gy", "gx"),
        P(("gx", "gy")),
        P("gx", "gy"),
        P(("gx", "gy")),
        P("gy", "gx"),
        P(("gx", "gy")),
        P("gx", "gy"),
        P(("gx", "gy")),
        P("gy", "gx"),
    )
    return jax.shard_map(
        local,
        mesh=mesh,
        in_specs=placed,
        out_specs=(
            P("gy", "gx"),
            P("gy", "gx"),
            P("gy"),
            P("gy"),
            P("gy"),
            P("gy"),
            P("gy", "gx"),
            P(("gx", "gy")),
            P("gx", "gy"),
            P(("gx", "gy")),
            P("gy", "gx"),
            P(("gx", "gy")),
            P("gx", "gy"),
            P(("gx", "gy")),
        ),
        check_vma=False,
    )
```

profile of v0, /device:TPU:13, one launch (start us, length us, event | category | flops | bytes accessed | tf_op | source)
XLA Modules:
  0.0 1941.3 jit_solution(1413502310639603368)
XLA Ops:
  13.1 12.0 all-reduce
  25.1 16.4 all-gather
  41.6 13.9 all-gather.1
  63.2 67.8 %all-gather.14.cloned.1.call-done = bf16[2048,1536]{1,0:T(8,128)(2,1)} async-done(((bf16[256,1536]{1,0:T(8,128)(2,1)}), bf16[2048,1536]{1,0:T(8,128)(2,1)}) %all-gather.14.cloned.1.call-update) | async-done | bytes 6291472 | tf_op jit(solution)/shard_map/all_gather | solution.py:142
  131.0 8.0 convolution_add_fusion
  165.1 35.5 %all-gather.2 = bf16[8,1,256]{2,1,0:T(2,128)(2,1)S(1)} all-gather(bf16[1,1,256]{2,1,0:T(2,128)(2,1)S(1)} %reshape.1499), channel_id=1, replica_groups=mesh['gx'=4,'gy'=8] {'gy'}, dimensions={0}, use_global_device_ids=true | all-gather | bytes 4608 | tf_op jit(solution)/shard_map/all_gather | solution.py:148
  200.6 13.4 all-gather.3
  214.0 15.4 all-gather.4
  252.4 29.0 %collective-permute-done.1 = bf16[2,512,512]{1,2,0:T(8,128)(2,1)} collective-permute-done((bf16[2,512,512]{1,2,0:T(8,128)(2,1)}, bf16[2,512,512]{1,2,0:T(8,128)(2,1)}, u32[]{:S(2)}, u32[]{:S(2)}) %collective-permute-start.1) | collective-permute-done | bytes 1048608 | tf_op jit(solution)/shard_map/ppermute | solution.py:17
  283.4 162.6 %collective-permute-done.2 = bf16[2,512,512]{1,2,0:T(8,128)(2,1)} collective-permute-done((bf16[2,512,512]{1,2,0:T(8,128)(2,1)}, bf16[2,512,512]{1,2,0:T(8,128)(2,1)}, u32[]{:S(2)}, u32[]{:S(2)}) %collective-permute-start.2) | collective-permute-done | bytes 1048608 | tf_op jit(solution)/shard_map/ppermute | solution.py:17
  451.4 32.0 %collective-permute-done.3 = bf16[2,512,512]{1,2,0:T(8,128)(2,1)} collective-permute-done((bf16[2,512,512]{1,2,0:T(8,128)(2,1)}, bf16[2,512,512]{1,2,0:T(8,128)(2,1)}, u32[]{:S(2)}, u32[]{:S(2)}) %collective-permute-start.3) | collective-permute-done | bytes 1048608 | tf_op jit(solution)/shard_map/ppermute | solution.py:17
  488.9 44.4 %collective-permute-start.10 = (bf16[4,512,512]{1,2,0:T(8,128)(2,1)}, bf16[4,512,512]{1,2,0:T(8,128)(2,1)}, u32[]{:S(2)}, u32[]{:S(2)}) collective-permute-start(bf16[4,512,512]{1,2,0:T(8,128)(2,1)} %pad_maximum_fusion), channel_id=1, source_target_pairs={{0,4},{1,5},{2,6},{3,7},{8,12},{9,13},{10,14},{11,15},{16,20},{17,... | collective-permute-start | bytes 6291464 | tf_op jit(solution)/shard_map/ppermute | solution.py:17
  578.1 214.2 %collective-permute-done.7 = bf16[4,512,512]{1,2,0:T(8,128)(2,1)} collective-permute-done((bf16[4,512,512]{1,2,0:T(8,128)(2,1)}, bf16[4,512,512]{1,2,0:T(8,128)(2,1)}, u32[]{:S(2)}, u32[]{:S(2)}) %collective-permute-start.7) | collective-permute-done | bytes 2097184 | tf_op jit(solution)/shard_map/ppermute | solution.py:17
  793.1 59.9 %collective-permute-done.9 = bf16[4,512,512]{1,2,0:T(8,128)(2,1)} collective-permute-done((bf16[4,512,512]{1,2,0:T(8,128)(2,1)}, bf16[4,512,512]{1,2,0:T(8,128)(2,1)}, u32[]{:S(2)}, u32[]{:S(2)}) %collective-permute-start.9) | collective-permute-done | bytes 2097184 | tf_op jit(solution)/shard_map/ppermute | solution.py:17
  855.0 52.7 %collective-permute-done.10 = bf16[4,512,512]{1,2,0:T(8,128)(2,1)} collective-permute-done((bf16[4,512,512]{1,2,0:T(8,128)(2,1)}, bf16[4,512,512]{1,2,0:T(8,128)(2,1)}, u32[]{:S(2)}, u32[]{:S(2)}) %collective-permute-start.10) | collective-permute-done | bytes 2097184 | tf_op jit(solution)/shard_map/ppermute | solution.py:17
  923.0 36.3 %collective-permute-done.8 = bf16[4,512,512]{1,2,0:T(8,128)(2,1)S(1)} collective-permute-done((bf16[4,512,512]{1,2,0:T(8,128)(2,1)}, bf16[4,512,512]{1,2,0:T(8,128)(2,1)S(1)}, u32[]{:S(2)}, u32[]{:S(2)}) %collective-permute-start.8) | collective-permute-done | bytes 2097184 | tf_op jit(solution)/shard_map/ppermute | solution.py:17
  962.1 25.0 %collective-permute-start.26 = (bf16[4,512,512]{1,2,0:T(8,128)(2,1)}, bf16[4,512,512]{1,2,0:T(8,128)(2,1)S(1)}, u32[]{:S(2)}, u32[]{:S(2)}) collective-permute-start(bf16[4,512,512]{1,2,0:T(8,128)(2,1)} %pad_maximum_fusion), channel_id=1, source_target_pairs={{1,0},{2,1},{3,2},{4,3},{5,4},{6,5},{7,6},{9,8},{10,9},{11,10},{12... | collective-permute-start | bytes 6291464 | tf_op jit(solution)/shard_map/ppermute | solution.py:17
  991.6 63.0 %collective-permute-done.20 = bf16[4,512,512]{1,2,0:T(8,128)(2,1)S(1)} collective-permute-done((bf16[4,512,512]{1,2,0:T(8,128)(2,1)}, bf16[4,512,512]{1,2,0:T(8,128)(2,1)S(1)}, u32[]{:S(2)}, u32[]{:S(2)}) %collective-permute-start.20) | collective-permute-done | bytes 2097184 | tf_op jit(solution)/shard_map/ppermute | solution.py:17
  1067.2 136.1 %collective-permute-done.24 = bf16[4,512,512]{1,2,0:T(8,128)(2,1)S(1)} collective-permute-done((bf16[4,512,512]{1,2,0:T(8,128)(2,1)}, bf16[4,512,512]{1,2,0:T(8,128)(2,1)S(1)}, u32[]{:S(2)}, u32[]{:S(2)}) %collective-permute-start.24) | collective-permute-done | bytes 2097184 | tf_op jit(solution)/shard_map/ppermute | solution.py:17
  1204.2 39.9 %collective-permute-done.26 = bf16[4,512,512]{1,2,0:T(8,128)(2,1)S(1)} collective-permute-done((bf16[4,512,512]{1,2,0:T(8,128)(2,1)}, bf16[4,512,512]{1,2,0:T(8,128)(2,1)S(1)}, u32[]{:S(2)}, u32[]{:S(2)}) %collective-permute-start.26) | collective-permute-done | bytes 2097184 | tf_op jit(solution)/shard_map/ppermute | solution.py:17
  1317.1 6.5 fusion.68
  1342.7 8.1 convolution_convert_fusion.5
  1350.8 9.6 fusion.383
  1360.4 19.3 fusion.389
  1401.0 7.3 convolution_convert_fusion.2
  1408.4 10.1 convolution_convert_fusion
  1418.8 8.7 convolution_convert_fusion.1
  1433.0 42.3 %all-reduce.14.cloned.1.call-done = (bf16[512,2048]{1,0:T(8,128)(2,1)}, bf16[512,2048]{1,0:T(8,128)(2,1)}) async-done(((bf16[512,2048]{1,0:T(8,128)(2,1)}, bf16[512,2048]{1,0:T(8,128)(2,1)}), (bf16[512,2048]{1,0:T(8,128)(2,1)}, bf16[512,2048]{1,0:T(8,128)(2,1)})) %all-reduce.14.cloned.1.call-update) | async-done | bytes 4194320 | tf_op jit(solution)/shard_map/psum | solution.py:299
  1483.6 23.9 %all-reduce.10 = (bf16[512]{0:T(512)(128)(2,1)S(1)}, bf16[512]{0:T(512)(128)(2,1)S(1)}, bf16[2048]{0:T(1024)(128)(2,1)S(1)}, bf16[2048]{0:T(1024)(128)(2,1)S(1)}...) all-reduce(bf16[512]{0:T(512)(128)(2,1)S(1)} %dynamic-update-slice., ...), channel_id=1, replica_groups=mesh['gx'=4,'gy'=8] {'gy'}, use_global_device_ids=true, to_apply=%add.2 | all-reduce | flops 13312 | bytes 53248
  1518.9 111.7 %reduce-scatter.8.cloned.1.call-done = bf16[256,1536]{1,0:T(8,128)(2,1)} async-done(((bf16[2048,1536]{1,0:T(8,128)(2,1)}), bf16[256,1536]{1,0:T(8,128)(2,1)}) %reduce-scatter.8.cloned.1.call-update) | async-done | bytes 786448 | tf_op jit(solution)/shard_map/reduce_scatter | solution.py:321
  1633.1 147.8 %reduce-scatter.14.cloned.1.call-done = bf16[2048,256]{1,0:T(8,128)(2,1)} async-done(((bf16[2048,2048]{1,0:T(8,128)(2,1)}), bf16[2048,256]{1,0:T(8,128)(2,1)}) %reduce-scatter.14.cloned.1.call-update) | async-done | bytes 1048592 | tf_op jit(solution)/shard_map/reduce_scatter | solution.py:244
  1783.5 147.4 %reduce-scatter.12.cloned.1.call-done = bf16[256,2048]{1,0:T(8,128)(2,1)} async-done(((bf16[2048,2048]{1,0:T(8,128)(2,1)}), bf16[256,2048]{1,0:T(8,128)(2,1)}) %reduce-scatter.12.cloned.1.call-update) | async-done | bytes 1048592 | tf_op jit(solution)/shard_map/reduce_scatter | solution.py:324
  (437 shorter events, 302.0 us)
Async XLA Ops:
  7.2 53.0 %all-gather.12.cloned.1.call-start = ((), (), s32[]{:S(2)}) async-start(), calls=%async_computation.5 | async-start | bytes 2621440 | tf_op jit(solution)/shard_map/all_gather | solution.py:140
  8.0 123.0 %all-gather.14.cloned.1.call-start = ((), (), s32[]{:S(2)}) async-start(), calls=%async_computation.6 | async-start | bytes 7077888 | tf_op jit(solution)/shard_map/all_gather | solution.py:142
  8.7 222.7 %all-gather.22.cloned.1.call-start = ((), (), s32[]{:S(2)}) async-start(), calls=%async_computation.11 | async-start | bytes 2621440 | tf_op jit(solution)/shard_map/all_gather | solution.py:233
  9.4 222.0 %all-gather.16.cloned.1.call-start = ((), (), s32[]{:S(2)}) async-start(), calls=%async_computation.7 | async-start | bytes 2359296 | tf_op jit(solution)/shard_map/all_gather | solution.py:211
  10.0 1340.8 %all-gather.18.cloned.1.call-start = ((), (), s32[]{:S(2)}) async-start(), calls=%async_computation.8 | async-start | bytes 9437184 | tf_op jit(solution)/shard_map/all_gather | solution.py:143
  10.6 1349.8 %all-gather.20.cloned.1.call-start = ((), (), s32[]{:S(2)}) async-start(), calls=%async_computation.9 | async-start | bytes 9437184 | tf_op jit(solution)/shard_map/all_gather | solution.py:212
  11.2 1420.0 %reduce-scatter.10.cloned.1.call-start = ((), (), s32[]{:S(2)}) async-start(), calls=%async_computation.13 | async-start | bytes 2359296 | tf_op jit(solution)/shard_map/reduce_scatter | solution.py:241
  157.4 93.0 %collective-permute-start = (bf16[2,512,512]{1,2,0:T(8,128)(2,1)}, bf16[2,512,512]{1,2,0:T(8,128)(2,1)}, u32[]{:S(2)}, u32[]{:S(2)}) collective-permute-start(bf16[2,512,512]{1,2,0:T(8,128)(2,1)} %pad_maximum_fusion.1), channel_id=1, source_target_pairs={{0,1},{1,2},{2,3},{3,4},{4,5},{5,6},{6,7},{8,9},{9,10},{10,11},{11... | collective-permute-start | bytes 3145736 | tf_op jit(solution)/shard_map/ppermute | solution.py:17
  236.1 209.9 %collective-permute-start.2 = (bf16[2,512,512]{1,2,0:T(8,128)(2,1)}, bf16[2,512,512]{1,2,0:T(8,128)(2,1)}, u32[]{:S(2)}, u32[]{:S(2)}) collective-permute-start(bf16[2,512,512]{1,2,0:T(8,128)(2,1)} %pad_maximum_fusion.1), channel_id=1, source_target_pairs={{0,3},{1,4},{2,5},{3,6},{4,7},{8,11},{9,12},{10,13},{11,14},{12,15... | collective-permute-start | bytes 3145736 | tf_op jit(solution)/shard_map/ppermute | solution.py:17
  238.8 244.6 %collective-permute-start.3 = (bf16[2,512,512]{1,2,0:T(8,128)(2,1)}, bf16[2,512,512]{1,2,0:T(8,128)(2,1)}, u32[]{:S(2)}, u32[]{:S(2)}) collective-permute-start(bf16[2,512,512]{1,2,0:T(8,128)(2,1)} %pad_maximum_fusion.1), channel_id=1, source_target_pairs={{0,4},{1,5},{2,6},{3,7},{8,12},{9,13},{10,14},{11,15},{16,20},{17,... | collective-permute-start | bytes 3145736 | tf_op jit(solution)/shard_map/ppermute | solution.py:17
  242.1 246.8 %collective-permute-start.4 = (bf16[2,512,512]{1,2,0:T(8,128)(2,1)}, bf16[2,512,512]{1,2,0:T(8,128)(2,1)}, u32[]{:S(2)}, u32[]{:S(2)}) collective-permute-start(bf16[2,512,512]{1,2,0:T(8,128)(2,1)} %pad_maximum_fusion.1), channel_id=1, source_target_pairs={{0,5},{1,6},{2,7},{8,13},{9,14},{10,15},{16,21},{17,22},{18,23},{2... | collective-permute-start | bytes 3145736 | tf_op jit(solution)/shard_map/ppermute | solution.py:17
  250.4 284.2 %collective-permute-start.5 = (bf16[2,512,512]{1,2,0:T(8,128)(2,1)}, bf16[2,512,512]{1,2,0:T(8,128)(2,1)S(1)}, u32[]{:S(2)}, u32[]{:S(2)}) collective-permute-start(bf16[2,512,512]{1,2,0:T(8,128)(2,1)} %pad_maximum_fusion.1), channel_id=1, source_target_pairs={{0,6},{1,7},{8,14},{9,15},{16,22},{17,23},{24,30},{25,31}} | collective-permute-start | bytes 3145736 | tf_op jit(solution)/shard_map/ppermute | solution.py:17
  281.4 253.3 %collective-permute-start.6 = (bf16[2,512,512]{1,2,0:T(8,128)(2,1)}, bf16[2,512,512]{1,2,0:T(8,128)(2,1)S(1)}, u32[]{:S(2)}, u32[]{:S(2)}) collective-permute-start(bf16[2,512,512]{1,2,0:T(8,128)(2,1)} %pad_maximum_fusion.1), channel_id=1, source_target_pairs={{0,7},{8,15},{16,23},{24,31}} | collective-permute-start | bytes 3145736 | tf_op jit(solution)/shard_map/ppermute | solution.py:17
  446.0 346.3 %collective-permute-start.7 = (bf16[4,512,512]{1,2,0:T(8,128)(2,1)}, bf16[4,512,512]{1,2,0:T(8,128)(2,1)}, u32[]{:S(2)}, u32[]{:S(2)}) collective-permute-start(bf16[4,512,512]{1,2,0:T(8,128)(2,1)} %pad_maximum_fusion), channel_id=1, source_target_pairs={{0,1},{1,2},{2,3},{3,4},{4,5},{5,6},{6,7},{8,9},{9,10},{10,11},{11... | collective-permute-start | bytes 6291464 | tf_op jit(solution)/shard_map/ppermute | solution.py:17
  483.4 369.6 %collective-permute-start.9 = (bf16[4,512,512]{1,2,0:T(8,128)(2,1)}, bf16[4,512,512]{1,2,0:T(8,128)(2,1)}, u32[]{:S(2)}, u32[]{:S(2)}) collective-permute-start(bf16[4,512,512]{1,2,0:T(8,128)(2,1)} %pad_maximum_fusion), channel_id=1, source_target_pairs={{0,3},{1,4},{2,5},{3,6},{4,7},{8,11},{9,12},{10,13},{11,14},{12,15... | collective-permute-start | bytes 6291464 | tf_op jit(solution)/shard_map/ppermute | solution.py:17
  488.9 418.7 %collective-permute-start.10 = (bf16[4,512,512]{1,2,0:T(8,128)(2,1)}, bf16[4,512,512]{1,2,0:T(8,128)(2,1)}, u32[]{:S(2)}, u32[]{:S(2)}) collective-permute-start(bf16[4,512,512]{1,2,0:T(8,128)(2,1)} %pad_maximum_fusion), channel_id=1, source_target_pairs={{0,4},{1,5},{2,6},{3,7},{8,12},{9,13},{10,14},{11,15},{16,20},{17,... | collective-permute-start | bytes 6291464 | tf_op jit(solution)/shard_map/ppermute | solution.py:17
  565.6 342.9 %collective-permute-start.11 = (bf16[4,512,512]{1,2,0:T(8,128)(2,1)}, bf16[4,512,512]{1,2,0:T(8,128)(2,1)}, u32[]{:S(2)}, u32[]{:S(2)}) collective-permute-start(bf16[4,512,512]{1,2,0:T(8,128)(2,1)} %pad_maximum_fusion), channel_id=1, source_target_pairs={{0,5},{1,6},{2,7},{8,13},{9,14},{10,15},{16,21},{17,22},{18,23},{2... | collective-permute-start | bytes 6291464 | tf_op jit(solution)/shard_map/ppermute | solution.py:17
  577.2 898.0 %all-reduce.14.cloned.1.call-start = ((), (), s32[]{:S(2)}) async-start(), calls=%async_computation.16 | async-start | bytes 8388608 | tf_op jit(solution)/shard_map/psum | solution.py:299
  577.3 336.4 %collective-permute-start.12 = (bf16[4,512,512]{1,2,0:T(8,128)(2,1)}, bf16[4,512,512]{1,2,0:T(8,128)(2,1)S(1)}, u32[]{:S(2)}, u32[]{:S(2)}) collective-permute-start(bf16[4,512,512]{1,2,0:T(8,128)(2,1)} %pad_maximum_fusion), channel_id=1, source_target_pairs={{0,6},{1,7},{8,14},{9,15},{16,22},{17,23},{24,30},{25,31}} | collective-permute-start | bytes 6291464 | tf_op jit(solution)/shard_map/ppermute | solution.py:17
  792.3 124.8 %collective-permute-start.13 = (bf16[4,512,512]{1,2,0:T(8,128)(2,1)}, bf16[4,512,512]{1,2,0:T(8,128)(2,1)S(1)}, u32[]{:S(2)}, u32[]{:S(2)}) collective-permute-start(bf16[4,512,512]{1,2,0:T(8,128)(2,1)} %pad_maximum_fusion), channel_id=1, source_target_pairs={{0,7},{8,15},{16,23},{24,31}} | collective-permute-start | bytes 6291464 | tf_op jit(solution)/shard_map/ppermute | solution.py:17
  853.1 106.2 %collective-permute-start.8 = (bf16[4,512,512]{1,2,0:T(8,128)(2,1)}, bf16[4,512,512]{1,2,0:T(8,128)(2,1)S(1)}, u32[]{:S(2)}, u32[]{:S(2)}) collective-permute-start(bf16[4,512,512]{1,2,0:T(8,128)(2,1)} %pad_maximum_fusion), channel_id=1, source_target_pairs={{0,2},{1,3},{2,4},{3,5},{4,6},{5,7},{8,10},{9,11},{10,12},{11,13},... | collective-permute-start | bytes 6291464 | tf_op jit(solution)/shard_map/ppermute | solution.py:17
  907.7 54.4 %collective-permute-start.14 = (bf16[4,512,512]{1,2,0:T(8,128)(2,1)}, bf16[4,512,512]{1,2,0:T(8,128)(2,1)S(1)}, u32[]{:S(2)}, u32[]{:S(2)}) collective-permute-start(bf16[4,512,512]{1,2,0:T(8,128)(2,1)} %pad_maximum_fusion), channel_id=1, source_target_pairs={{7,0},{15,8},{23,16},{31,24}} | collective-permute-start | bytes 6291464 | tf_op jit(solution)/shard_map/ppermute | solution.py:17
  908.5 79.4 %collective-permute-start.18 = (bf16[4,512,512]{1,2,0:T(8,128)(2,1)}, bf16[4,512,512]{1,2,0:T(8,128)(2,1)S(1)}, u32[]{:S(2)}, u32[]{:S(2)}) collective-permute-start(bf16[4,512,512]{1,2,0:T(8,128)(2,1)} %pad_maximum_fusion), channel_id=1, source_target_pairs={{5,0},{6,1},{7,2},{13,8},{14,9},{15,10},{21,16},{22,17},{23,18},{2... | collective-permute-start | bytes 6291464 | tf_op jit(solution)/shard_map/ppermute | solution.py:17
  913.7 140.9 %collective-permute-start.20 = (bf16[4,512,512]{1,2,0:T(8,128)(2,1)}, bf16[4,512,512]{1,2,0:T(8,128)(2,1)S(1)}, u32[]{:S(2)}, u32[]{:S(2)}) collective-permute-start(bf16[4,512,512]{1,2,0:T(8,128)(2,1)} %pad_maximum_fusion), channel_id=1, source_target_pairs={{4,0},{5,1},{6,2},{7,3},{12,8},{13,9},{14,10},{15,11},{20,16},{21,... | collective-permute-start | bytes 6291464 | tf_op jit(solution)/shard_map/ppermute | solution.py:17
  917.1 138.4 %collective-permute-start.22 = (bf16[4,512,512]{1,2,0:T(8,128)(2,1)}, bf16[4,512,512]{1,2,0:T(8,128)(2,1)S(1)}, u32[]{:S(2)}, u32[]{:S(2)}) collective-permute-start(bf16[4,512,512]{1,2,0:T(8,128)(2,1)} %pad_maximum_fusion), channel_id=1, source_target_pairs={{3,0},{4,1},{5,2},{6,3},{7,4},{11,8},{12,9},{13,10},{14,11},{15,12... | collective-permute-start | bytes 6291464 | tf_op jit(solution)/shard_map/ppermute | solution.py:17
  959.3 244.1 %collective-permute-start.24 = (bf16[4,512,512]{1,2,0:T(8,128)(2,1)}, bf16[4,512,512]{1,2,0:T(8,128)(2,1)S(1)}, u32[]{:S(2)}, u32[]{:S(2)}) collective-permute-start(bf16[4,512,512]{1,2,0:T(8,128)(2,1)} %pad_maximum_fusion), channel_id=1, source_target_pairs={{2,0},{3,1},{4,2},{5,3},{6,4},{7,5},{10,8},{11,9},{12,10},{13,11},... | collective-permute-start | bytes 6291464 | tf_op jit(solution)/shard_map/ppermute | solution.py:17
  962.1 282.0 %collective-permute-start.26 = (bf16[4,512,512]{1,2,0:T(8,128)(2,1)}, bf16[4,512,512]{1,2,0:T(8,128)(2,1)S(1)}, u32[]{:S(2)}, u32[]{:S(2)}) collective-permute-start(bf16[4,512,512]{1,2,0:T(8,128)(2,1)} %pad_maximum_fusion), channel_id=1, source_target_pairs={{1,0},{2,1},{3,2},{4,3},{5,4},{6,5},{7,6},{9,8},{10,9},{11,10},{12... | collective-permute-start | bytes 6291464 | tf_op jit(solution)/shard_map/ppermute | solution.py:17
  987.9 267.5 %collective-permute-start.16 = (bf16[4,512,512]{1,2,0:T(8,128)(2,1)}, bf16[4,512,512]{1,2,0:T(8,128)(2,1)S(1)}, u32[]{:S(2)}, u32[]{:S(2)}) collective-permute-start(bf16[4,512,512]{1,2,0:T(8,128)(2,1)} %pad_maximum_fusion), channel_id=1, source_target_pairs={{6,0},{7,1},{14,8},{15,9},{22,16},{23,17},{30,24},{31,25}} | collective-permute-start | bytes 6291464 | tf_op jit(solution)/shard_map/ppermute | solution.py:17
  1386.8 130.1 %reduce-scatter.6.cloned.1.call-start = ((), (), s32[]{:S(2)}) async-start(), calls=%async_computation.10 | async-start | bytes 2621440 | tf_op jit(solution)/shard_map/reduce_scatter | solution.py:224
  1400.3 230.3 %reduce-scatter.8.cloned.1.call-start = ((), (), s32[]{:S(2)}) async-start(), calls=%async_computation.12 | async-start | bytes 7077888 | tf_op jit(solution)/shard_map/reduce_scatter | solution.py:321
  1408.4 372.5 %reduce-scatter.14.cloned.1.call-start = ((), (), s32[]{:S(2)}) async-start(), calls=%async_computation.15 | async-start | bytes 9437184 | tf_op jit(solution)/shard_map/reduce_scatter | solution.py:244
  1418.6 512.4 %reduce-scatter.12.cloned.1.call-start = ((), (), s32[]{:S(2)}) async-start(), calls=%async_computation.14 | async-start | bytes 9437184 | tf_op jit(solution)/shard_map/reduce_scatter | solution.py:324
  (93 other events, 3521.2 us)
Sparse Core Ops, SparseCore 0:
  9.6 24.0 all-gather.11
  35.9 95.0 all-gather.13
  132.5 24.4 all-gather.21
  158.9 53.7 all-gather.15
  214.7 258.8 all-gather.17
  475.5 348.3 all-gather.19
  827.4 333.3 reduce-scatter.9
  1386.9 88.2 all-reduce.13
  1478.4 31.4 reduce-scatter.5
  1513.3 117.2 reduce-scatter.7
  1634.2 146.5 reduce-scatter.13
  1784.3 146.5 reduce-scatter.11
where the time goes:
time: 1950 us; the launch traced here: 1940 us
  waiting for transfers between devices  1350 us (69%)
  matrix products  205 us (11%)
  blocking collectives  130 us (7%)
  starting transfers between devices  119 us (6%)
  other arithmetic  62.8 us (3%)
  local copies, waits for them, and re-layouts  58.4 us (3%)
    ppermute x28, waiting for transfers between devices, passed_along(): lax.ppermute(value, axis, [(source, source + steps) for source in range(l...  826 us
    reduce_scatter x1, waiting for transfers between devices, local(): lax.psum_scatter(grad_down_local.astype(jnp.bfloat16), 'gy', scatter_dime...  148 us
    reduce_scatter x1, waiting for transfers between devices, local(): lax.psum_scatter(grad_up_local.astype(jnp.bfloat16), 'gy', scatter_dimens...  147 us
    ppermute x28, starting transfers between devices, passed_along(): lax.ppermute(value, axis, [(source, source + steps) for source in range(l...  117 us
    reduce_scatter x1, waiting for transfers between devices, local(): lax.psum_scatter(grad_qkv_local.astype(jnp.bfloat16), 'gy', scatter_dimen...  112 us
    all_gather x1, waiting for transfers between devices, local(): lax.all_gather(qkv_weight, 'gy', axis=0, tiled=True)  67.8 us
    psum x1, waiting for transfers between devices, local(): lax.psum(grad_norm_ffn.astype(jnp.bfloat16), 'gx').astype(jnp.float32)  42.3 us
  transfers between devices with their start and end apart: 40, of which 15 were waited for; matrix products, arithmetic and copies ran while one was open for 16% of the time, Pallas kernels for 0%

commit v1 on v0

--- a/solution.py
+++ b/solution.py
@@ -1,6 +1,8 @@
 import jax
 import jax.numpy as jnp
 from jax import lax
+from jax.experimental import pallas as pl
+from jax.experimental.pallas import tpu as pltpu
 from jax.sharding import PartitionSpec as P
 
 HEAD = 256
@@ -361,6 +363,1120 @@
     )
 
 
+MESH = pl.DeviceIdType.MESH
+NX = 4
+NY = 8
+
+
+class Place:
+    def __init__(self):
+        self.gx, self.gy = lax.axis_index("gx"), lax.axis_index("gy")
+        self.z, self.y = self.gy // 2, self.gy % 2
+        self.near = self.gx + 1 - 2 * (self.gx % 2)
+        self.far = (self.gx + 2) % NX
+        self.over = (self.near + 2) % NX
+        self.side = self.gy + 1 - 2 * self.y
+
+    def up(self, step):
+        return ((self.z + step) % 4) * 2 + self.y
+
+
+class Post:
+    def __init__(self, send, recv):
+        self.send, self.recv, self.used = send, recv, 0
+        self.open = []
+
+    def take(self, count=1):
+        first = self.used
+        self.used += count
+        return first
+
+    def copy(self, slot, src, dst, gx, gy, offset=None):
+        index = slot if offset is None else slot + offset
+        return pltpu.make_async_remote_copy(
+            src_ref=src,
+            dst_ref=dst,
+            send_sem=self.send.at[slot],
+            recv_sem=self.recv.at[index],
+            device_id=(gx, gy),
+            device_id_type=MESH,
+        )
+
+    def go(self, *args, **kw):
+        made = self.copy(*args, **kw)
+        made.start()
+        self.open.append(made)
+        return made
+
+    def arrived(self, slot, dst, gx, gy):
+        self.copy(slot, dst, dst, gx, gy).wait_recv()
+
+    def close(self):
+        for made in self.open:
+            made.wait_send()
+        self.open = []
+
+
+def greet(peers):
+    barrier = pltpu.get_barrier_semaphore()
+    for gx, gy in peers:
+        pl.semaphore_signal(barrier, inc=1, device_id=(gx, gy), device_id_type=MESH)
+    pl.semaphore_wait(barrier, len(peers))
+
+
+def greet_all(here):
+    barrier = pltpu.get_barrier_semaphore()
+    gx, gy = here.gx, here.gy
+    peers = [((gx + s) % NX, gy) for s in range(1, NX)]
+    peers += [(gx, (gy + s) % NY) for s in range(1, NY)]
+    for px, py in peers:
+        pl.semaphore_signal(barrier, inc=1, device_id=(px, py), device_id_type=MESH)
+    peers = [(here.z, 2 * gx), (here.z, 2 * gx + 1)]
+    for px, py in peers:
+        pl.semaphore_signal(barrier, inc=1, device_id=(px, py), device_id_type=MESH)
+    pl.semaphore_wait(barrier, NX + NY)
+    return here.z == gx
+
+
+def row_spread(post, here, src, dst, local_sem):
+    sub, part = dst.shape[0], src.shape[1]
+    slot = post.take(NX)
+    own = pltpu.make_async_copy(
+        src.at[pl.ds(pl.multiple_of(here.gx * sub, sub), sub)],
+        dst.at[:, pl.ds(pl.multiple_of(here.gx * part, part), part)],
+        local_sem,
+    )
+    own.start()
+    for step in range(1, NX):
+        to = (here.gx + step) % NX
+        post.go(
+            slot + step,
+            src.at[pl.ds(pl.multiple_of(to * sub, sub), sub)],
+            dst.at[:, pl.ds(pl.multiple_of(here.gx * part, part), part)],
+            to,
+            here.gy,
+        )
+
+    def wait():
+        own.wait()
+        for step in range(1, NX):
+            came = (here.gx + NX - step) % NX
+            post.arrived(
+                slot + step, dst.at[:, pl.ds(pl.multiple_of(came * part, part), part)], came, here.gy
+            )
+
+    return wait
+
+
+def small_spread(post, here, src, dst, local_sem):
+    part = src.shape[1]
+    slot = post.take(NX)
+    mine = dst.at[:, pl.ds(pl.multiple_of(here.gx * part, part), part)]
+    own = pltpu.make_async_copy(src, mine, local_sem)
+    own.start()
+    for step in range(1, NX):
+        post.go(slot + step, src, mine, (here.gx + step) % NX, here.gy)
+
+    def wait():
+        own.wait()
+        for step in range(1, NX):
+            came = (here.gx + NX - step) % NX
+            post.arrived(
+                slot + step, dst.at[:, pl.ds(pl.multiple_of(came * part, part), part)], came, here.gy
+            )
+
+    return wait
+
+
+def line_gather(post, here, blocks):
+    ups, downs, ys = post.take(3), post.take(3), post.take(7)
+    z, y, gx = here.z, here.y, here.gx
+
+    def at(line):
+        return blocks.at[line * 2 + y]
+
+    def send(step, way, wait):
+        line = z - way * step
+        first = ups if way > 0 else downs
+        made = post.copy(first + step, at(line), at(line), gx, (z + way) * 2 + y)
+        ok = jnp.logical_and(
+            jnp.logical_and(line >= 0, line <= 3), (z < 3) if way > 0 else (z > 0)
+        )
+
+        @pl.when(ok)
+        def _():
+            made.wait_send() if wait else made.start()
+
+    def come(step, way):
+        line = z - way * step
+        first = ups if way > 0 else downs
+        made = post.copy(first + step - 1, at(line), at(line), gx, here.side)
+        on = post.copy(ys + 2 * step - (way > 0), at(line), at(line), gx, here.side)
+        ok = (line >= 0) if way > 0 else (line <= 3)
+
+        @pl.when(ok)
+        def _():
+            made.wait_recv()
+            on.start()
+
+    own = post.copy(ys, at(z), at(z), gx, here.side)
+    send(0, 1, False)
+    send(0, -1, False)
+    own.start()
+
+    def relay(step):
+        come(step, 1)
+        come(step, -1)
+        if step < 3:
+            send(step, 1, False)
+            send(step, -1, False)
+
+    def wait():
+        own.wait_send()
+        post.copy(ys, at(z), blocks.at[here.side], gx, here.side).wait_recv()
+        for step in (0, 1, 2):
+            send(step, 1, True)
+            send(step, -1, True)
+        for step in (1, 2, 3):
+            for way in (1, -1):
+                line = z - way * step
+                ok = (line >= 0) if way > 0 else (line <= 3)
+                slot = ys + 2 * step - (way > 0)
+
+                @pl.when(ok)
+                def _():
+                    post.copy(slot, at(line), at(line), gx, here.side).wait_send()
+                    post.copy(
+                        slot, at(line), blocks.at[line * 2 + 1 - y], gx, here.side
+                    ).wait_recv()
+
+    return relay, wait
+
+
+def gather_kernel(tok, small, cot, qkv, outw, up, down, xb, cb, wq, wo, uu, dd, send, recv, fsend, frecv, loc):
+    here = Place()
+    post = Post(send, recv)
+    gx, gy = here.gx, here.gy
+    width3 = wq.shape[2]
+    head = wo.shape[1]
+    unit = uu.shape[2]
+    selfish = greet_all(here)
+    sub = cb.shape[1]
+    tok_wait = row_spread(post, here, tok, xb.at[gy, 0:sub], loc.at[0])
+    small_wait = small_spread(post, here, small, xb.at[gy, sub : sub + 16], loc.at[1])
+    att = post.take(4)
+    for t in (0, 1):
+        alone = jnp.logical_and(selfish, here.y == t)
+        for k, (src, dst) in enumerate(
+            (
+                (qkv.at[:, t * width3 : (t + 1) * width3], wq.at[gy]),
+                (outw.at[t * head : (t + 1) * head, :], wo.at[gy]),
+            )
+        ):
+            @pl.when(alone)
+            def _():
+                pltpu.make_async_copy(src, dst, loc.at[2 + k]).start()
+
+            @pl.when(jnp.logical_not(alone))
+            def _():
+                pltpu.make_async_remote_copy(
+                    src_ref=src,
+                    dst_ref=dst,
+                    send_sem=send.at[att + 2 * t + k],
+                    recv_sem=recv.at[att + 2 * here.y + k],
+                    device_id=(here.z, 2 * gx + t),
+                    device_id_type=MESH,
+                ).start()
+    cot_wait = row_spread(post, here, cot, cb.at[gy], loc.at[4])
+    tok_wait()
+    small_wait()
+    tok_relay, tok_done = line_gather(post, here, xb)
+    for t in (0, 1):
+        alone = jnp.logical_and(selfish, here.y == t)
+        for k, (src, dst) in enumerate(
+            (
+                (qkv.at[:, t * width3 : (t + 1) * width3], wq),
+                (outw.at[t * head : (t + 1) * head, :], wo),
+            )
+        ):
+            @pl.when(alone)
+            def _():
+                pltpu.make_async_copy(src, dst.at[gy], loc.at[2 + k]).wait()
+
+            @pl.when(jnp.logical_not(alone))
+            def _():
+                slot = dst.at[2 * gx + t]
+                made = pltpu.make_async_remote_copy(
+                    src_ref=src,
+                    dst_ref=slot,
+                    send_sem=send.at[att + 2 * t + k],
+                    recv_sem=recv.at[att + 2 * t + k],
+                    device_id=(here.z, 2 * gx + t),
+                    device_id_type=MESH,
+                )
+                made.wait_send()
+                made.wait_recv()
+    att_far, att_near, att_over = post.take(2), post.take(2), post.take(2)
+    for k, w in enumerate((wq, wo)):
+        pair = w.at[pl.ds(2 * gx, 2)]
+        post.go(att_far + k, pair, pair, here.far, gy)
+        post.go(att_near + k, pair, pair, here.near, gy)
+    for hop in (1, 2, 3):
+        tok_relay(hop)
+    mine_u = uu.at[gx]
+    mine_d = dd.at[gx]
+    own_u = pltpu.make_async_copy(
+        up.at[:, pl.ds(pl.multiple_of(gy * unit, unit), unit)],
+        mine_u.at[pl.ds(pl.multiple_of(gy * unit, unit), unit)],
+        loc.at[5],
+    )
+    own_d = pltpu.make_async_copy(
+        down.at[pl.ds(pl.multiple_of(gy * unit, unit), unit), :],
+        mine_d.at[:, pl.ds(pl.multiple_of(gy * unit, unit), unit)],
+        loc.at[6],
+    )
+    own_u.start()
+    own_d.start()
+
+    def ffn(k, step, to):
+        place = pl.ds(pl.multiple_of(gy * unit, unit), unit)
+        theirs = pl.ds(pl.multiple_of(to * unit, unit), unit)
+        src = up.at[:, theirs] if k == 0 else down.at[theirs, :]
+        dst = mine_u.at[place] if k == 0 else mine_d.at[:, place]
+        return pltpu.make_async_remote_copy(
+            src_ref=src, dst_ref=dst, send_sem=fsend.at[k, step], recv_sem=frecv.at[k, gy],
+            device_id=(gx, to), device_id_type=MESH,
+        )
+
+    for step in range(1, NY):
+        for k in (0, 1):
+            ffn(k, step, (gy + step) % NY).start()
+    cot_wait()
+    cot_relay, cot_done = line_gather(post, here, cb)
+    for k, w in enumerate((wq, wo)):
+        pair = w.at[pl.ds(2 * here.far, 2)]
+        post.arrived(att_far + k, pair, here.far, gy)
+        post.go(att_over + k, pair, pair, here.near, gy)
+
+    def piece(k, part, q):
+        place = pl.ds(pl.multiple_of(q * unit, unit), unit)
+        return uu.at[part, place] if k == 0 else dd.at[part, :, place]
+
+    def pass_on(k, row, part, q, to):
+        ref = piece(k, part, q)
+        return pltpu.make_async_remote_copy(
+            src_ref=ref, dst_ref=ref, send_sem=fsend.at[row, q], recv_sem=frecv.at[row, q],
+            device_id=(to, gy), device_id_type=MESH,
+        )
+
+    own_u.wait()
+    own_d.wait()
+
+    def first(q, carried):
+        for k in (0, 1):
+            @pl.when(q != gy)
+            def _():
+                ref = piece(k, gx, q)
+                pltpu.make_async_remote_copy(
+                    src_ref=ref, dst_ref=ref, send_sem=fsend.at[k, 0], recv_sem=frecv.at[k, q],
+                    device_id=(gx, q), device_id_type=MESH,
+                ).wait_recv()
+            pass_on(k, 2 + k, gx, q, here.far).start()
+            pass_on(k, 4 + k, gx, q, here.near).start()
+        return carried
+
+    lax.fori_loop(0, NY, first, 0)
+    cot_relay(1)
+    cot_relay(2)
+
+    def second(q, carried):
+        for k in (0, 1):
+            pass_on(k, 2 + k, here.far, q, here.far).wait_recv()
+            pass_on(k, 6 + k, here.far, q, here.near).start()
+        return carried
+
+    cot_relay(3)
+    lax.fori_loop(0, NY, second, 0)
+    tok_done()
+    cot_done()
+    for k, w in enumerate((wq, wo)):
+        post.arrived(att_near + k, w.at[pl.ds(2 * here.near, 2)], here.near, gy)
+        post.arrived(att_over + k, w.at[pl.ds(2 * here.over, 2)], here.near, gy)
+
+    def third(q, carried):
+        for k in (0, 1):
+            pass_on(k, 4 + k, here.near, q, here.near).wait_recv()
+            pass_on(k, 6 + k, here.over, q, here.near).wait_recv()
+            pass_on(k, 2 + k, gx, q, here.far).wait_send()
+            pass_on(k, 4 + k, gx, q, here.near).wait_send()
+            pass_on(k, 6 + k, here.far, q, here.near).wait_send()
+        return carried
+
+    lax.fori_loop(0, NY, third, 0)
+    for step in range(1, NY):
+        for k in (0, 1):
+            ffn(k, step, (gy + step) % NY).wait_send()
+    post.close()
+
+
+def gather_all(tokens, small, cotangent, qkv_weight, out_weight, up_weight, down_weight):
+    block_rows, part = tokens.shape
+    sub = block_rows // NX
+    width = part * NX
+    krows = qkv_weight.shape[0]
+    bf16 = jnp.bfloat16
+    unit = up_weight.shape[1] // NY
+    vm = pl.BlockSpec(memory_space=pltpu.VMEM)
+    hb = pl.BlockSpec(memory_space=pl.ANY)
+    return pl.pallas_call(
+        gather_kernel,
+        out_shape=[
+            jax.ShapeDtypeStruct((NY, sub + 16, width), bf16),
+            jax.ShapeDtypeStruct((NY, sub, width), bf16),
+            jax.ShapeDtypeStruct((NY, krows, qkv_weight.shape[1] // 2), bf16),
+            jax.ShapeDtypeStruct((NY, out_weight.shape[0] // 2, out_weight.shape[1]), bf16),
+            jax.ShapeDtypeStruct((NX, width, unit), bf16),
+            jax.ShapeDtypeStruct((NX, unit, width), bf16),
+        ],
+        in_specs=[hb] * 7,
+        out_specs=[vm] * 6,
+        scratch_shapes=[
+            pltpu.SemaphoreType.DMA((48,)),
+            pltpu.SemaphoreType.DMA((48,)),
+            pltpu.SemaphoreType.DMA((8, 8)),
+            pltpu.SemaphoreType.DMA((8, 8)),
+            pltpu.SemaphoreType.DMA((8,)),
+        ],
+        compiler_params=pltpu.CompilerParams(
+            collective_id=0, has_side_effects=True, vmem_limit_bytes=50 * 2**20
+        ),
+        name="gather_all",
+    )(tokens, small, cotangent, qkv_weight, out_weight, up_weight, down_weight)
+
+
+def over_rows(count, width, fn):
+    chunk = 16
+    while 2 * chunk * width <= 65536 and count % (2 * chunk) == 0:
+        chunk *= 2
+
+    def body(index, carried):
+        fn(pl.ds(pl.multiple_of(index * chunk, chunk), chunk))
+        return carried
+
+    lax.fori_loop(0, count // chunk, body, 0)
+
+
+def shifted(rows, offset):
+    return pl.ds(pl.multiple_of(rows.start + offset, 16), rows.size)
+
+
+class Reduce:
+    def __init__(self, post, here, load, full, near, mine, sent, came):
+        self.post, self.here = post, here
+        self.near, self.mine, self.sent, self.came = near, mine, sent, came
+        self.rows, self.width = sent.shape
+        self.slot = post.take(2)
+        self.far = post.take(1)
+        rows = self.rows
+        group = lambda p: full.at[pl.ds(pl.multiple_of(p * rows, rows), rows)]
+        for k, p in enumerate((here.near, here.over)):
+            post.go(self.slot + k, group(p), near.at[k * rows : (k + 1) * rows], here.near, here.gy)
+        self.loads = [
+            load(group(p), mine.at[k * rows : (k + 1) * rows])
+            for k, p in enumerate((here.gx, here.far))
+        ]
+
+    def cross(self):
+        rows = self.rows
+        self.loads[1].wait()
+        self.post.arrived(
+            self.slot + 1, self.near.at[rows : 2 * rows], self.here.near, self.here.gy
+        )
+
+        def add(r):
+            low = shifted(r, rows)
+            self.sent[r] = (
+                self.mine[low].astype(jnp.float32) + self.near[low].astype(jnp.float32)
+            ).astype(jnp.bfloat16)
+
+        over_rows(rows, self.width, add)
+        self.post.go(self.far, self.sent, self.came, self.here.far, self.here.gy)
+
+    def total(self, put):
+        rows = self.rows
+        self.loads[0].wait()
+        self.post.arrived(self.slot, self.near.at[0:rows], self.here.near, self.here.gy)
+        self.post.arrived(self.far, self.came, self.here.far, self.here.gy)
+
+        def add(r):
+            put(
+                r,
+                self.mine[r].astype(jnp.float32)
+                + self.near[r].astype(jnp.float32)
+                + self.came[r].astype(jnp.float32),
+            )
+
+        over_rows(rows, self.width, add)
+
+
+def scatter_kernel(
+    bo, ug, dq, do, qb, du, dd, ub, own, tok, cot, cols,
+    output, grad_tokens, gains, smalls, gup, gdown, gqkv, gout, gqb, gub,
+    half, come, stage, uhalf, ucome, ustage,
+    nq, no, nqb, nu, nd, nub, kq, ko, kqb, ku, kd, kub, fq, fo, fqb, fu, fd, fub,
+    rq, ro, rqb, ru, rd, rub, au, ad, aq, ao, ab, mixed, mixed_land, back, back_land,
+    send, recv, fsend, frecv, loc,
+):
+    here = Place()
+    gx, gy, z, y = here.gx, here.gy, here.z, here.y
+    post = Post(send, recv)
+    f32, bf16 = jnp.float32, jnp.bfloat16
+    selfish = greet_all(here)
+    locs = [0]
+
+    def load(src, dst):
+        made = pltpu.make_async_copy(src, dst, loc.at[locs[0]])
+        locs[0] += 1
+        made.start()
+        return made
+
+    def reduce(*refs):
+        return Reduce(post, here, load, *refs)
+
+    red_q = reduce(dq, nq, kq, fq, rq)
+    red_o = reduce(do, no, ko, fo, ro)
+    red_b = reduce(qb, nqb, kqb, fqb, rqb)
+    red_u = reduce(du, nu, ku, fu, ru)
+    red_d = reduce(dd, nd, kd, fd, rd)
+    red_c = reduce(ub, nub, kub, fub, rub)
+    ys = []
+    for src, mine, land in ((bo, half, come), (ug, uhalf, ucome)):
+        slot = post.take(4)
+        for k in range(4):
+            post.go(slot + k, src.at[2 * k + 1 - y], land.at[k], gx, here.side)
+        ys.append((slot, [load(src.at[2 * k + y], mine.at[k]) for k in range(4)]))
+    for red in (red_q, red_o, red_b, red_u, red_d, red_c):
+        red.cross()
+
+    zs = []
+    for (slot, made), mine, land, arrive in (
+        (ys[0], half, come, stage),
+        (ys[1], uhalf, ucome, ustage),
+    ):
+        for k in range(4):
+            made[k].wait()
+            post.arrived(slot + k, land.at[k], gx, here.side)
+        first = post.take(4)
+        zs.append(first)
+        rows, width = mine.shape[1:]
+        for step in (1, 2, 3):
+            to = (z + step) % 4
+
+            def add(r):
+                mine[to, r] = (mine[to, r].astype(f32) + land[to, r].astype(f32)).astype(bf16)
+
+            over_rows(rows, width, add)
+            post.go(first + step, mine.at[to], arrive.at[step - 1], gx, to * 2 + y)
+
+    for red, keep in ((red_q, kq), (red_o, ko), (red_b, kqb)):
+
+        def put(r, value):
+            keep[r] = value.astype(bf16)
+
+        red.total(put)
+    att = post.take(6)
+    trio = ((kq, aq), (ko, ao), (kqb, ab))
+
+    def row_pair(ref, t, out):
+        rows = out.shape[1]
+        return ref.at[t * rows : (t + 1) * rows]
+
+    for t in (0, 1):
+        alone = jnp.logical_and(selfish, y == t)
+        for k, (mine, out) in enumerate(trio):
+
+            @pl.when(alone)
+            def _():
+                made = pltpu.make_async_copy(row_pair(mine, t, out), out.at[t], loc.at[40 + k])
+                made.start()
+                made.wait()
+
+            @pl.when(jnp.logical_not(alone))
+            def _():
+                pltpu.make_async_remote_copy(
+                    src_ref=row_pair(mine, t, out), dst_ref=out.at[y],
+                    send_sem=send.at[att + 3 * t + k], recv_sem=recv.at[att + 3 * y + k],
+                    device_id=(z, 2 * gx + t), device_id_type=MESH,
+                ).start()
+
+    unit = au.shape[0]
+    place = pl.ds(pl.multiple_of(gy * unit, unit), unit)
+    for k, (red, mine) in enumerate(((red_u, ku), (red_d, kd))):
+
+        def put(r, value):
+            mine[r] = value.astype(bf16)
+
+        red.total(put)
+        for step in range(1, NY):
+            to = (gy + step) % NY
+            theirs = pl.ds(pl.multiple_of(to * unit, unit), unit)
+            pltpu.make_async_remote_copy(
+                src_ref=mine.at[theirs] if k == 0 else mine.at[0:unit, theirs],
+                dst_ref=au.at[:, place] if k == 0 else ad.at[place],
+                send_sem=fsend.at[k, step], recv_sem=frecv.at[k, step],
+                device_id=(gx, to), device_id_type=MESH,
+            ).start()
+        if k == 0:
+            gup[:, place] = mine[place].astype(f32)
+        else:
+            gdown[place] = mine[0:unit, place].astype(f32)
+
+    def put_b(r, value):
+        gub[r] = value
+
+    red_c.total(put_b)
+
+    sub, width = own.shape
+    part = width // NX
+
+    def summed(n, mine, land, arrive, r):
+        total = mine[z, r].astype(f32) + land[z, r].astype(f32)
+        for step in (1, 2, 3):
+            total = total + arrive[step - 1, r].astype(f32)
+        return total
+
+    def await_z(n, arrive):
+        for step in (1, 2, 3):
+            post.arrived(zs[n] + step, arrive.at[step - 1], gx, ((z + 4 - step) % 4) * 2 + y)
+
+    await_z(0, stage)
+
+    def put_mixed(r):
+        total = summed(0, half, come, stage, r).astype(bf16)
+        for p in range(NX):
+            mixed[p, r] = total[:, p * part : (p + 1) * part]
+
+    over_rows(sub, 4 * width, put_mixed)
+    xs = post.take(4)
+    for step in range(1, NX):
+        to = (gx + step) % NX
+        post.go(xs + step, mixed.at[to], mixed_land.at[step - 1], to, gy)
+    await_z(1, ustage)
+
+    def put_back(r):
+        rows = summed(1, uhalf, ucome, ustage, r)
+        tokens = own[r].astype(f32)
+        centred = tokens - jnp.mean(tokens, axis=-1, keepdims=True)
+        rate = lax.rsqrt(jnp.mean(centred * centred, axis=-1, keepdims=True) + eps_norm)
+        xhat = centred * rate
+        grads = rate * (
+            rows
+            - jnp.mean(rows, axis=-1, keepdims=True)
+            - xhat * jnp.mean(rows * xhat, axis=-1, keepdims=True)
+        )
+        grads = grads.astype(bf16)
+        for p in range(NX):
+            back[p, r] = grads[:, p * part : (p + 1) * part]
+
+    over_rows(sub, 4 * width, put_back)
+    rest = summed(1, uhalf, ucome, ustage, pl.ds(sub, 16))
+    smalls[...] = rest
+    low = rest.astype(bf16)
+    for p in range(NX):
+        for q in (0, 1):
+            back[p, sub + 16 * q : sub + 16 * (q + 1)] = low[:, q * part : (q + 1) * part]
+    us = post.take(4)
+    for step in range(1, NX):
+        to = (gx + step) % NX
+        post.go(us + step, back.at[to], back_land.at[step - 1], to, gy)
+
+    def rows_of(p):
+        return pl.multiple_of(p * sub, sub)
+
+    def put_output(p, block):
+        def put(r):
+            there = shifted(r, rows_of(p))
+            output[there] = (tok[there].astype(f32) + block[r].astype(f32) + cols[...]).astype(bf16)
+
+        over_rows(sub, 2 * part, put)
+
+    put_output(gx, mixed.at[gx])
+    for step in range(1, NX):
+        came = (gx + NX - step) % NX
+        post.arrived(xs + step, mixed_land.at[step - 1], came, gy)
+        put_output(came, mixed_land.at[step - 1])
+
+    for t in (0, 1):
+        alone = jnp.logical_and(selfish, y == t)
+        for k, (mine, out) in enumerate(trio):
+
+            @pl.when(jnp.logical_not(alone))
+            def _():
+                made = pltpu.make_async_remote_copy(
+                    src_ref=row_pair(mine, t, out), dst_ref=out.at[t],
+                    send_sem=send.at[att + 3 * t + k], recv_sem=recv.at[att + 3 * t + k],
+                    device_id=(z, 2 * gx + t), device_id_type=MESH,
+                )
+                made.wait_send()
+                made.wait_recv()
+
+    krows, wide = aq.shape[1:]
+    head = ao.shape[1]
+    for a in (0, 1):
+
+        def put_q(r):
+            gqkv[r, a * wide : (a + 1) * wide] = aq[a, r].astype(f32)
+            gout[shifted(r, a * head)] = ao[a, r].astype(f32)
+
+        over_rows(krows, 2 * wide, put_q)
+        gqb[a] = ab[a].astype(f32)
+    for k in (0, 1):
+        for step in range(1, NY):
+            came = (gy + NY - step) % NY
+            theirs = pl.ds(pl.multiple_of(came * unit, unit), unit)
+            ref = au.at[:, theirs] if k == 0 else ad.at[theirs]
+            made = pltpu.make_async_remote_copy(
+                src_ref=ref, dst_ref=ref, send_sem=fsend.at[k, step], recv_sem=frecv.at[k, step],
+                device_id=(gx, came), device_id_type=MESH,
+            )
+            made.wait_send()
+            made.wait_recv()
+            if k == 0:
+                gup[:, theirs] = au[:, theirs].astype(f32)
+            else:
+                gdown[theirs] = ad[theirs].astype(f32)
+
+    def put_grad(p, block):
+        def put(r):
+            there = shifted(r, rows_of(p))
+            grad_tokens[there] = cot[there].astype(f32) + block[r].astype(f32)
+
+        over_rows(sub, 2 * part, put)
+
+    put_grad(gx, back.at[gx])
+    tail = back[gx, sub : sub + 32].astype(f32)
+    for step in range(1, NX):
+        came = (gx + NX - step) % NX
+        post.arrived(us + step, back_land.at[step - 1], came, gy)
+        put_grad(came, back_land.at[step - 1])
+        tail = tail + back_land[step - 1, sub : sub + 32].astype(f32)
+    gains[...] = tail
+    post.close()
+
+
+def scatter_all(bo, ug, dq, do, qb, du, dd, ub, own, tok, cot, cols):
+    bf16, f32 = jnp.bfloat16, jnp.float32
+    sub, width = own.shape
+    part = width // NX
+    krows = dq.shape[0] // NY
+    wide = dq.shape[1]
+    unit = du.shape[1]
+    head = do.shape[1]
+    S = jax.ShapeDtypeStruct
+    V = pltpu.VMEM
+    vm = pl.BlockSpec(memory_space=pltpu.VMEM)
+    hb = pl.BlockSpec(memory_space=pl.ANY)
+    six = [(a.shape[0] // NX, a.shape[1]) for a in (dq, do, qb, du, dd, ub)]
+    return pl.pallas_call(
+        scatter_kernel,
+        out_shape=[
+            S((NX * sub, part), bf16),
+            S((NX * sub, part), f32),
+            S((32, part), f32),
+            S((16, width), f32),
+            S((krows, NY * unit), f32),
+            S((NY * unit, krows), f32),
+            S((krows, 2 * wide), f32),
+            S((2 * head, krows), f32),
+            S((2, 16, qb.shape[1]), f32),
+            S((16, unit), f32),
+        ],
+        in_specs=[hb] * 8 + [vm] * 4,
+        out_specs=[vm] * 10,
+        scratch_shapes=[
+            V((4, sub, width), bf16), V((4, sub, width), bf16), V((3, sub, width), bf16),
+            V((4, sub + 16, width), bf16), V((4, sub + 16, width), bf16), V((3, sub + 16, width), bf16),
+        ]
+        + [V((2 * r, c), bf16) for r, c in six]
+        + [V((2 * r, c), bf16) for r, c in six]
+        + [V((r, c), bf16) for r, c in six]
+        + [V((r, c), bf16) for r, c in six]
+        + [
+            V((krows, NY * unit), bf16), V((NY * unit, krows), bf16), V((2, krows, wide), bf16),
+            V((2, krows, head), bf16), V((2, 16, qb.shape[1]), bf16),
+            V((NX, sub, part), bf16), V((NX - 1, sub, part), bf16),
+            V((NX, sub + 32, part), bf16), V((NX - 1, sub + 32, part), bf16),
+            pltpu.SemaphoreType.DMA((64,)), pltpu.SemaphoreType.DMA((64,)),
+            pltpu.SemaphoreType.DMA((2, 8)), pltpu.SemaphoreType.DMA((2, 8)),
+            pltpu.SemaphoreType.DMA((48,)),
+        ],
+        compiler_params=pltpu.CompilerParams(
+            collective_id=1, has_side_effects=True, vmem_limit_bytes=60 * 2**20
+        ),
+        name="scatter_all",
+    )(bo, ug, dq, do, qb, du, dd, ub, own, tok, cot, cols)
+
+
+def chunk_mask(sub, gx, tile, chunk, queries, keys):
+    row = lax.broadcasted_iota(jnp.int32, (queries, keys), 0)
+    col = lax.broadcasted_iota(jnp.int32, (queries, keys), 1)
+    span = NX * sub
+    query_pos = span * (2 * tile + row // sub) + sub * gx + row % sub
+    return span * chunk + col <= query_pos
+
+
+def load_chunk(sub, parts, chunk, low, high):
+    rows = pl.ds(pl.multiple_of(chunk * sub, sub), sub)
+    return jnp.concatenate([parts[p, rows, low:high] for p in range(NX)], axis=0)
+
+
+def attend_tile(sub, gx, tile, q, parts, ctx, low, log):
+    rows = 2 * sub
+    place = pl.ds(pl.multiple_of(tile * rows, rows), rows)
+    query = q[place]
+
+    def step(chunk, carried, masked):
+        top, total, summed = carried
+        keys = load_chunk(sub, parts, chunk, 0, HEAD)
+        values = load_chunk(sub, parts, chunk, HEAD, 2 * HEAD)
+        scores = contract_last(query, keys)
+        if masked:
+            visible = chunk_mask(sub, gx, tile, chunk, rows, NX * sub)
+            scores = jnp.where(visible, scores, -1e30)
+        new_top = jnp.maximum(top, jnp.max(scores, axis=-1, keepdims=True))
+        weights = jnp.exp(scores - new_top)
+        if masked:
+            weights = jnp.where(visible, weights, 0.0)
+        shrink = jnp.exp(top - new_top)
+        total = total * shrink + jnp.sum(weights, axis=-1, keepdims=True)
+        summed = summed * shrink + jnp.dot(
+            weights.astype(jnp.bfloat16), values, preferred_element_type=jnp.float32
+        )
+        return new_top, total, summed
+
+    state = (
+        jnp.full((rows, 1), -1e30, jnp.float32),
+        jnp.zeros((rows, 1), jnp.float32),
+        jnp.zeros((rows, HEAD), jnp.float32),
+    )
+    state = lax.fori_loop(0, 2 * tile, lambda c, s: step(c, s, False), state)
+    state = step(2 * tile, state, True)
+    state = step(2 * tile + 1, state, True)
+    top, total, summed = state
+    context = summed / total
+    ctx[place] = context
+    low[place] = context.astype(jnp.bfloat16)
+    log[place] = jnp.broadcast_to(top + jnp.log(total), (rows, log.shape[1]))
+
+
+def attend_kernel(q, kv, ctx, low, log, parts, send, recv, loc):
+    here = Place()
+    gx, gy = here.gx, here.gy
+    post = Post(send, recv)
+    sub = q.shape[0] // NY
+    greet([(here.near, gy), (here.far, gy)])
+    own = pltpu.make_async_copy(kv, parts.at[gx], loc.at[0])
+    own.start()
+    slot = post.take(3)
+    post.go(slot, kv, parts.at[gx], here.far, gy)
+    post.go(slot + 1, kv, parts.at[gx], here.near, gy)
+    post.arrived(slot, parts.at[here.far], here.far, gy)
+    post.go(slot + 2, parts.at[here.far], parts.at[here.far], here.near, gy)
+    own.wait()
+    post.arrived(slot + 1, parts.at[here.near], here.near, gy)
+    post.arrived(slot + 2, parts.at[here.over], here.near, gy)
+
+    def tile(t, carried):
+        attend_tile(sub, gx, t, q, parts, ctx, low, log)
+        return carried
+
+    lax.fori_loop(0, NY // 2, tile, 0)
+    post.close()
+
+
+def attend(query, kv):
+    rows = query.shape[0]
+    S = jax.ShapeDtypeStruct
+    vm = pl.BlockSpec(memory_space=pltpu.VMEM)
+    return pl.pallas_call(
+        attend_kernel,
+        out_shape=[
+            S((rows, HEAD), jnp.float32),
+            S((rows, HEAD), jnp.bfloat16),
+            S((rows, 128), jnp.float32),
+            S((NX,) + kv.shape, jnp.bfloat16),
+        ],
+        in_specs=[vm] * 2,
+        out_specs=[vm] * 4,
+        scratch_shapes=[pltpu.SemaphoreType.DMA((8,)), pltpu.SemaphoreType.DMA((8,)), pltpu.SemaphoreType.DMA((2,))],
+        compiler_params=pltpu.CompilerParams(collective_id=2, has_side_effects=True, vmem_limit_bytes=32 * 2**20),
+        name="attend",
+    )(query, kv)
+
+
+def attend_back_tile(sub, gx, tile, q, g, ctx, log, parts, dq, acc):
+    rows = 2 * sub
+    place = pl.ds(pl.multiple_of(tile * rows, rows), rows)
+    query = q[place]
+    grad = g[place]
+    log_total = log[place, 0:1]
+    delta = jnp.sum(grad.astype(jnp.float32) * ctx[place], axis=-1, keepdims=True)
+
+    def step(chunk, carried, masked):
+        keys = load_chunk(sub, parts, chunk, 0, HEAD)
+        values = load_chunk(sub, parts, chunk, HEAD, 2 * HEAD)
+        probs = contract_last(query, keys) - log_total
+        if masked:
+            visible = chunk_mask(sub, gx, tile, chunk, rows, NX * sub)
+            probs = jnp.where(visible, jnp.exp(jnp.where(visible, probs, 0.0)), 0.0)
+        else:
+            probs = jnp.exp(probs)
+        grad_probs = contract_last(grad, values)
+        grad_scores = (probs * (grad_probs - delta)).astype(jnp.bfloat16)
+        acc[chunk, :, 0:HEAD] += contract_first(grad_scores, query)
+        acc[chunk, :, HEAD : 2 * HEAD] += contract_first(probs.astype(jnp.bfloat16), grad)
+        return carried + jnp.dot(grad_scores, keys, preferred_element_type=jnp.float32)
+
+    total = jnp.zeros((rows, HEAD), jnp.float32)
+    total = lax.fori_loop(0, 2 * tile, lambda c, s: step(c, s, False), total)
+    total = step(2 * tile, total, True)
+    total = step(2 * tile + 1, total, True)
+    dq[place] = total * HEAD ** (-0.5)
+
+
+def attend_back_kernel(
+    q, g, ctx, log, parts, dq, dkv, acc, low, near, mine, sent, came, send, recv, loc
+):
+    here = Place()
+    gx, gy = here.gx, here.gy
+    post = Post(send, recv)
+    sub = q.shape[0] // NY
+    greet([(here.near, gy), (here.far, gy)])
+
+    def clear(chunk, carried):
+        acc[chunk] = jnp.zeros(acc.shape[1:], jnp.float32)
+        return carried
+
+    lax.fori_loop(0, NY, clear, 0)
+
+    def tile(t, carried):
+        attend_back_tile(sub, gx, t, q, g, ctx, log, parts, dq, acc)
+        return carried
+
+    lax.fori_loop(0, NY // 2, tile, 0)
+
+    def flush(chunk, carried):
+        for p in range(NX):
+            low[pl.ds(pl.multiple_of(p * sub * NY + chunk * sub, sub), sub)] = acc[
+                chunk, p * sub : (p + 1) * sub
+            ].astype(jnp.bfloat16)
+        return carried
+
+    lax.fori_loop(0, NY, flush, 0)
+    locs = [0]
+
+    def load(src, dst):
+        made = pltpu.make_async_copy(src, dst, loc.at[locs[0]])
+        locs[0] += 1
+        made.start()
+        return made
+
+    red = Reduce(post, here, load, low, near, mine, sent, came)
+    red.cross()
+
+    def put(r, value):
+        dkv[r] = value
+
+    red.total(put)
+    post.close()
+
+
+def attend_back(query, grad, context, log_total, parts):
+    rows = query.shape[0]
+    sub = rows // NY
+    S, V = jax.ShapeDtypeStruct, pltpu.VMEM
+    bf16 = jnp.bfloat16
+    vm = pl.BlockSpec(memory_space=pltpu.VMEM)
+    width = 2 * HEAD
+    return pl.pallas_call(
+        attend_back_kernel,
+        out_shape=[S((rows, HEAD), jnp.float32), S((rows, width), jnp.float32)],
+        in_specs=[vm] * 5,
+        out_specs=[vm] * 2,
+        scratch_shapes=[
+            V((NY, NX * sub, width), jnp.float32), V((NX * rows, width), bf16),
+            V((2 * rows, width), bf16), V((2 * rows, width), bf16), V((rows, width), bf16), V((rows, width), bf16),
+            pltpu.SemaphoreType.DMA((8,)), pltpu.SemaphoreType.DMA((8,)), pltpu.SemaphoreType.DMA((2,)),
+        ],
+        compiler_params=pltpu.CompilerParams(collective_id=3, has_side_effects=True, vmem_limit_bytes=48 * 2**20),
+        name="attend_back",
+    )(query, grad, context, log_total, parts)
+
+
+def regroup(
+    tokens,
+    attn_gain,
+    attn_shift,
+    ffn_gain,
+    ffn_shift,
+    qkv_weight,
+    qkv_bias,
+    out_weight,
+    out_bias,
+    up_weight,
+    up_bias,
+    down_weight,
+    down_bias,
+    cotangent,
+):
+    f32, bf16 = jnp.float32, jnp.bfloat16
+    gx, gy = lax.axis_index("gx"), lax.axis_index("gy")
+    nx, ny = NX, NY
+    block_rows, part = tokens.shape
+    width = nx * part
+    sub = block_rows // nx
+    rows = sub * ny
+    unit = up_weight.shape[1] // ny
+    krows = qkv_weight.shape[0]
+    head_cols = 3 * HEAD
+
+    def line(*pieces):
+        flat = jnp.concatenate(pieces)
+        return jnp.pad(flat, (0, part - flat.shape[0]))[None]
+
+    small = jnp.concatenate(
+        [
+            line(attn_gain, attn_shift),
+            line(ffn_gain, ffn_shift),
+            line(up_bias, qkv_bias),
+            line(out_bias, down_bias),
+            jnp.zeros((12, part), bf16),
+        ]
+    )
+    xb, cb, wq, wo, uu, dd = gather_all(
+        tokens, small, cotangent, qkv_weight, out_weight, up_weight, down_weight
+    )
+    cot = cb.reshape(rows, width)
+    qkv_full = wq.reshape(width, head_cols)
+    out_full = jnp.transpose(wo, (1, 0, 2)).reshape(HEAD, width)
+    up_full = jnp.transpose(uu, (1, 0, 2)).reshape(width, nx * unit)
+    down_full = dd.reshape(nx * unit, width)
+
+    lines = xb[:, sub : sub + 4].reshape(ny, 4, nx, part).astype(f32)
+    gain_attn = lines[:, 0, 0, :krows].reshape(1, width)
+    shift_attn = lines[:, 0, 0, krows:].reshape(1, width)
+    gain_ffn = lines[:, 1, 0, :krows].reshape(1, width)
+    shift_ffn = lines[:, 1, 0, krows:].reshape(1, width)
+    up_shift = lax.dynamic_index_in_dim(lines[:, 2, :, :unit], gy, 0, keepdims=False).reshape(-1)
+    bias_size = qkv_bias.shape[0]
+    qkv_all = jnp.transpose(lines[:, 2, :, unit : unit + bias_size], (1, 0, 2)).reshape(
+        ny, head_cols
+    )
+    qkv_shift = lax.dynamic_index_in_dim(qkv_all, gy, 0, keepdims=False)
+    mine = lax.dynamic_index_in_dim(lines[:, 3], gx, 1, keepdims=False)
+    size = out_bias.shape[0]
+    out_cols = mine[:, :size].reshape(1, part) + mine[:, size : 2 * size].reshape(1, part)
+
+    full_rows = xb[:, :sub].reshape(rows, width).astype(f32)
+    average = jnp.mean(full_rows, axis=-1, keepdims=True)
+    centred = full_rows - average
+    rate = lax.rsqrt(jnp.mean(centred * centred, axis=-1, keepdims=True) + eps_norm)
+    xhat = centred * rate
+    normed_attn = (xhat * gain_attn + shift_attn).astype(bf16)
+    normed_ffn = (xhat * gain_ffn + shift_ffn).astype(bf16)
+
+    position = (
+        block_rows * jnp.arange(ny, dtype=jnp.int32)[:, None]
+        + sub * gx
+        + jnp.arange(sub, dtype=jnp.int32)[None]
+    ).reshape(rows)
+    angles = angle_table(position)
+    mixed = jnp.dot(normed_attn, qkv_full, preferred_element_type=f32) + qkv_shift
+    mixed = mixed.reshape(rows, 1, 3, HEAD)
+    query = (rotate(mixed[:, :, 0], angles).astype(bf16) * jnp.asarray(HEAD ** (-0.5), bf16)).reshape(
+        rows, HEAD
+    )
+    key = rotate(mixed[:, :, 1], angles).astype(bf16).reshape(rows, HEAD)
+    value = mixed[:, :, 2].astype(bf16).reshape(rows, HEAD)
+    context, context_low, log_total, kv_parts = attend(query, jnp.concatenate([key, value], axis=1))
+
+    hidden_pre = jnp.dot(normed_ffn, up_full, preferred_element_type=f32) + up_shift
+    hidden, gelu_back = jax.vjp(exact_gelu, hidden_pre)
+    hidden_low = hidden.astype(bf16)
+    branch = jnp.dot(hidden_low, down_full, preferred_element_type=f32) + jnp.dot(
+        context_low, out_full, preferred_element_type=f32
+    )
+    branch = branch.astype(bf16).reshape(ny, sub, width)
+
+    grad_context = contract_last(cot, out_full).astype(bf16)
+    grad_hidden = contract_last(cot, down_full)
+    grad_pre = gelu_back(grad_hidden)[0].astype(bf16)
+    dq, dkv = attend_back(query, grad_context, context, log_total, kv_parts)
+    spun = [
+        unrotate(g.reshape(rows, 1, HEAD), angles).reshape(rows, HEAD) for g in (dq, dkv[:, :HEAD])
+    ]
+    grad_mixed = jnp.concatenate(spun + [dkv[:, HEAD:]], axis=1).astype(bf16)
+
+    d_up = jnp.concatenate(
+        [
+            contract_first(normed_ffn, grad_pre[:, p * unit : (p + 1) * unit]).astype(bf16)
+            for p in range(nx)
+        ]
+    )
+    d_down = contract_first(hidden_low, cot).astype(bf16)
+    d_up_b = jnp.sum(grad_pre.astype(f32), axis=0).astype(bf16).reshape(nx, 1, unit)
+    ub = jnp.pad(d_up_b, ((0, 0), (0, 15), (0, 0))).reshape(nx * 16, unit)
+    d_qkv = contract_first(normed_attn, grad_mixed).astype(bf16)
+    d_out = contract_first(context_low, cot).astype(bf16)
+    d_out = jnp.transpose(d_out.reshape(HEAD, ny, krows), (1, 0, 2)).reshape(ny * HEAD, krows)
+    d_qkv_b = jnp.sum(grad_mixed.astype(f32), axis=0).astype(bf16).reshape(4, 1, bias_size)
+    qb = jnp.pad(
+        jnp.concatenate([d_qkv_b, d_qkv_b]), ((0, 0), (0, 15), (0, krows - bias_size))
+    ).reshape(ny * 16, krows)
+
+    grad_norm_attn = contract_last(grad_mixed, qkv_full)
+    grad_norm_ffn = contract_last(grad_pre, up_full)
+    u = (grad_norm_attn * gain_attn + grad_norm_ffn * gain_ffn).astype(bf16)
+    sums = jnp.stack(
+        [
+            jnp.sum(grad_norm_attn * xhat, axis=0),
+            jnp.sum(grad_norm_attn, axis=0),
+            jnp.sum(grad_norm_ffn * xhat, axis=0),
+            jnp.sum(grad_norm_ffn, axis=0),
+        ]
+    ).reshape(4, ny, krows)
+    cot_sum = jnp.sum(cotangent.astype(f32), axis=0).reshape(1, ny, size)
+    cot_sum = jnp.pad(cot_sum, ((0, 0), (0, 0), (0, krows - size)))
+    rest = jnp.concatenate([sums, cot_sum, jnp.zeros((3, ny, krows), f32)])
+    rest = jnp.transpose(rest, (1, 0, 2)).reshape(ny, 1, width).astype(bf16)
+    ug = jnp.concatenate(
+        [u.reshape(ny, sub, width), jnp.pad(rest, ((0, 0), (0, 15), (0, 0)))], axis=1
+    )
+    own = lax.dynamic_index_in_dim(xb, gy, 0, keepdims=False)[:sub]
+    output, grad_tokens, gains, smalls, gup, gdown, gqkv, gout, gqb, gub = scatter_all(
+        branch, ug, d_qkv, d_out, qb, d_up, d_down, ub, own, tokens, cotangent, out_cols
+    )
+    gain_sum = gains.reshape(2, 16, part)[:, 0].reshape(4, krows)
+    grad_bias = smalls[0, 4 * krows : 4 * krows + size]
+    grad_qkv_b = jnp.where(gy < 4, gqb[0, 0], gqb[1, 0])[:bias_size]
+    return (
+        output,
+        grad_tokens,
+        gain_sum[0],
+        gain_sum[1],
+        gain_sum[2],
+        gain_sum[3],
+        gqkv,
+        grad_qkv_b,
+        gout,
+        grad_bias,
+        gup,
+        gub[0],
+        gdown,
+        grad_bias,
+    )
+
+
 def solution(mesh):
     placed = (
         P("gy", "gx"),
@@ -379,7 +1495,7 @@
         P("gy", "gx"),
     )
     return jax.shard_map(
-        local,
+        regroup if mesh.shape["gy"] == NY == SPAN and mesh.shape["gx"] == NX else local,
         mesh=mesh,
         in_specs=placed,
         out_specs=(

time: 1950 us -> 698 us (0.36)
  waiting for transfers between devices: 1350 us -> 0 us
  Pallas kernels: 0 us -> 531 us
  blocking collectives: 130 us -> 0 us
  matrix products: 205 us -> 79.9 us
  starting transfers between devices: 119 us -> 0 us
  other arithmetic: 62.8 us -> 32.1 us
    ppermute x28 -> x0, waiting for transfers between devices: 826 us -> none  [passed_along(): lax.ppermute(value, axis, [(source, source + steps) for source in range(l...]
    pallas_call x0 -> x4, Pallas kernels: none -> 531 us  [the longest x1 251 us: scatter_all(): pl.pallas_call(scatter_kernel, out_shape=[S((NX * sub, part), bf16), S((N...]
    reduce_scatter x5 -> x0, waiting for transfers between devices: 407 us -> none  [the longest x1 148 us: local(): lax.psum_scatter(grad_down_local.astype(jnp.bfloat16), 'gy', scatter_dime...]
    dot_general x59 -> x4, matrix products: 139 us -> 19.8 us  [the longest x1 6.36 us: regroup(): jnp.dot(hidden_low, down_full, preferred_element_type=f32)]
    ppermute x28 -> x0, starting transfers between devices: 117 us -> none  [passed_along(): lax.ppermute(value, axis, [(source, source + steps) for source in range(l...]
    all_gather x5 -> x0, blocking collectives: 94.6 us -> none  [the longest x1 35.5 us: local(): lax.all_gather(ffn_gain, 'gy', axis=0, tiled=True)]
    all_gather x6 -> x0, waiting for transfers between devices: 67.8 us -> none  [the longest x1 67.8 us: local(): lax.all_gather(qkv_weight, 'gy', axis=0, tiled=True)]
    psum x1 -> x0, waiting for transfers between devices: 42.3 us -> none  [local(): lax.psum(grad_norm_ffn.astype(jnp.bfloat16), 'gx').astype(jnp.float32)]
  transfers between devices with their start and end apart: 40 -> 0, of which waited for: 15 -> 0; matrix products, arithmetic and copies ran while one was open for 16% -> 0% of each run, Pallas kernels for 0% -> 0%
where the time goes in v1:
time: 698 us; the launch traced here: 689 us
  Pallas kernels  531 us (76%)
  matrix products  79.9 us (11%)
  local copies, waits for them, and re-layouts  43.8 us (6%)
  other arithmetic  32.1 us (5%)
    pallas_call x1, Pallas kernels, scatter_all(): pl.pallas_call(scatter_kernel, out_shape=[S((NX * sub, part), bf16), S((N...  251 us
    pallas_call x1, Pallas kernels, gather_all(): pl.pallas_call(gather_kernel, out_shape=[jax.ShapeDtypeStruct((NY, sub +...  190 us
    pallas_call x1, Pallas kernels, attend_back(): pl.pallas_call(attend_back_kernel, out_shape=[S((rows, HEAD), jnp.float32...  50.1 us
    pallas_call x1, Pallas kernels, attend(): pl.pallas_call(attend_kernel, out_shape=[S((rows, HEAD), jnp.float32), S(...  40.2 us
    dot_general x4, matrix products, contract_last(): lax.dot_general(left, right, (((1,), (1,)), ((), ())), preferred_element_...  39.9 us
    unnamed x71, local copies, waits for them, and re-layouts  23.2 us
    dot_general x7, matrix products, contract_first(): lax.dot_general(left, right, (((0,), (0,)), ((), ())), preferred_element_...  20.2 us

profile of v1, /device:TPU:13, one launch (start us, length us, event | category | flops | bytes accessed | tf_op | source)
XLA Modules:
  0.0 688.6 jit_solution(10086194871151231356)
XLA Ops:
  9.2 190.2 %gather_all.1 = (bf16[8,144,2048]{2,1,0:T(8,128)(2,1)}, bf16[8,128,2048]{2,1,0:T(8,128)(2,1)}, bf16[8,256,768]{2,1,0:T(8,128)(2,1)}, bf16[8,256,256]{2,1,0:T(8,1...) custom-call(bf16[512,512]{1,0:T(8,128)(2,1)S(1)} %copy-done.2, ...), custom_call_target="tpu_custom_call" | custom-call | tf_op jit(solution)/shard_map/gather_all/pallas_call | solution.py:731
  199.4 6.3 copy.44
  205.8 2.8 convert_reduce_fusion
  208.6 3.0 multiply_reduce_fusion.2
  213.8 1.9 dynamic-slice_bitcast_fusion.own
  216.2 3.8 convolution_convert_fusion.7.g
  220.0 4.5 add_convert_fusion.4
  224.6 3.6 convolution_add_fusion
  228.2 6.4 fusion.69
  239.2 1.6 copy.65
  240.7 2.5 fusion.48
  244.7 40.2 %attend.1 = (f32[1024,256]{1,0:T(8,128)S(1)}, bf16[1024,256]{1,0:T(8,128)(2,1)S(1)}, f32[1024,128]{1,0:T(8,128)S(1)}, bf16[4,1024,512]{2,1,0:T(8,128)(2,1)S(1)}) custom-call(bf16[1024,256]{1,0:T(8,128)(2,1)S(1)} %maximum_multiply_fusion.q, bf16[1024,512]{1,0:T(8,128)(2,1)S(1)} %pad_maximum_fusion.2.kv), custom_call_target="tpu_custom_call" | custom-call | tf_op jit(solution)/shard_map/attend/pallas_call | solution.py:1201
  284.9 2.0 copy-done.1
  286.9 50.1 %attend_back.1 = (f32[1024,256]{1,0:T(8,128)S(1)}, f32[1024,512]{1,0:T(8,128)S(1)}) custom-call(bf16[1024,256]{1,0:T(8,128)(2,1)S(1)} %maximum_multiply_fusion.q, bf16[1024,256]{1,0:T(8,128)(2,1)S(1)} %convolution_convert_fusion.7.g, f32[1024,256]{1,0:T(8,128)S(1)} %get-tuple-element.43.ctx, f32[1024,128]{1,0:T(8,128)S(1)} %get-tuple-element.44.log, ...), custom_call_target="tpu_custom_call" | custom-call | tf_op jit(solution)/shard_map/attend_back/pallas_call | solution.py:1301
  337.4 2.5 fusion.34
  342.2 3.6 convolution_convert_fusion.6
  346.9 16.9 %fusion.63 = (bf16[1024]{0:T(1024)(128)(2,1)S(1)}, bf16[1024,1024]{1,0:T(8,128)(2,1)}, f32[1024,1024]{1,0:T(8,128)S(1)}) fusion(f32[1024,1024]{1,0:T(8,128)S(1)} %copy-done.5, f32[1024]{0:T(1024)S(1)} %bitcast.150, bf16[1024,2048]{1,0:T(8,128)(2,1)} %bitcast.163, bf16[1024,2048]{1,0:T(8,128)(2,1)S(1)} %bitcast.160), kind=kOutput, calls=%fused_computation.132 | convolution fusion | flops 4372560896 | bytes 18880512 | tf_op jit(solution)/shard_map/dot_general | solution.py:72
  366.0 6.2 convolution_convert_fusion.dd
  372.8 6.4 fusion.70
  379.2 3.5 add_convert_fusion.3
  383.2 6.7 fusion.71
  389.9 12.5 %fusion.62 = (bf16[2048]{0:T(1024)(128)(2,1)S(1)}, bf16[2048]{0:T(1024)(128)(2,1)S(1)}, bf16[1024,2048]{1,0:T(8,128)(2,1)}, bf16[2048]{0:T(1024)(128)(2,1)S(1)},...) fusion(f32[1024]{0:T(1024)S(1)} %get-tuple-element.98, ...), kind=kOutput, calls=%fused_computation.131 | convolution fusion | flops 3265781760 | bytes 29941760 | tf_op jit(solution)/shard_map/dot_general | solution.py:72
  402.6 5.2 fusion.2.ug
  410.6 1.4 convolution_convert_fusion.4
  412.0 1.4 convolution_convert_fusion.5
  413.4 2.3 pad_maximum_fusion.du
  415.7 1.4 copy-done.25
  417.1 4.9 convolution_convert_fusion.1.dq
  421.9 250.8 %scatter_all.1 = (bf16[512,512]{1,0:T(8,128)(2,1)}, f32[512,512]{1,0:T(8,128)}, f32[32,512]{1,0:T(8,128)}, f32[16,2048]{1,0:T(8,128)}, f32[256,2048]{1,0:T(8,128...) custom-call(bf16[8,128,2048]{2,1,0:T(8,128)(2,1)} %bitcast.119, ...), custom_call_target="tpu_custom_call" | custom-call | tf_op jit(solution)/shard_map/scatter_all/pallas_call | solution.py:1080
  678.0 1.9 copy.84
  679.9 2.3 copy.85
  682.1 2.8 copy.86
  (131 shorter events, 35.7 us)
Async XLA Ops:
  5.0 1.0 copy-start
  6.1 1.0 copy-start.2
  7.1 1.1 copy-start.3
  8.2 0.9 copy-start.4
  216.2 8.3 %copy-start.6 = (bf16[256,8,256]{0,2,1:T(8,128)(2,1)}, bf16[256,8,256]{0,2,1:T(8,128)(2,1)S(1)}, u32[]{:S(2)}) copy-start(bf16[256,8,256]{0,2,1:T(8,128)(2,1)S(1)} %copy.50) | copy-start | bytes 3145732
  220.0 4.5 copy-start.20
  224.6 3.6 copy-start.8
  240.7 3.3 copy-start.10
  284.8 2.0 copy-start.1
  341.1 4.7 copy-start.13
  341.1 4.7 copy-start.15
  342.2 4.7 copy-start.5
  342.2 4.7 copy-start.18
  363.9 2.2 copy-start.19
  372.8 6.4 copy-start.7
  379.2 3.6 copy-start.9
  379.2 4.0 copy-start.23
  379.2 10.6 %slice-start = ((s8[4718592]{0:T(1024)(128)(4,1)}), s8[4194304]{0:T(1024)(128)(4,1)S(1)}, s32[]{:S(2)}) async-start(s8[4718592]{0:T(1024)(128)(4,1)} %bitcast.117), calls=%async_computation | async-start | bytes 8388608
  383.2 6.7 slice-start.1
  383.2 6.7 copy-start.14
  383.2 6.7 copy-start.16
  402.6 5.3 copy-start.22
  402.6 5.3 copy-start.24
  413.4 3.7 copy-start.25
  672.7 12.2 %copy-start.17 = (f32[512,256]{1,0:T(8,128)S(1)}, f32[512,256]{1,0:T(8,128)}, u32[]{:S(2)}) copy-start(f32[512,256]{1,0:T(8,128)} %get-tuple-element.152) | copy-start | bytes 1572868
  672.7 13.0 %copy-start.12 = (f32[256,2048]{1,0:T(8,128)S(1)}, f32[256,2048]{1,0:T(8,128)}, u32[]{:S(2)}) copy-start(f32[256,2048]{1,0:T(8,128)} %get-tuple-element.154) | copy-start | bytes 6291460
  673.6 13.5 %copy-start.21 = (f32[64]{0:T(128)}, f32[64]{0:T(128)S(1)}, u32[]{:S(2)}) copy-start(f32[64]{0:T(128)S(1)} %slice_bitcast_fusion.1) | copy-start | bytes 772
  682.1 4.9 copy-start.11
